TPU v7x, 32 devices: a whole 2x2x4 slice. The times are simulated.
32 devices in a mesh: wide: 16 (over z, x, core), grp: 2 (over y).
Axes of the slice: x: 2, y: 2, z: 4, core: 2. Of those that a mesh axis runs over, the one named last changes fastest.
Arguments:
- fields: float32 [256, 8, 4096], P('wide', None, 'grp'), may hold values from -6 to 6
- slot_mask: int32 [256, 8], P('wide'), may hold values 0 or 1
- noise_step: int32 [256], P('wide'), may hold values from 0 to 999
- cotangent: bfloat16 [256, 128, 4096], P('wide', 'grp'), may hold values from -6 to 6
- in_weight: float32 [72, 128], replicated, may hold values from -0.75 to 0.75
- in_moment: float32 [72, 128], replicated, may hold values from -6144 to 6144
- in_square: float32 [72, 128], replicated, may hold values from 524288 to 8388608
- mid_weight: float32 [2304, 128], P(('wide', 'grp')), may hold values from -0.1875 to 0.1875
- mid_moment: float32 [2304, 128], P(('wide', 'grp')), may hold values from -2560 to 2560
- mid_square: float32 [2304, 128], P(('wide', 'grp')), may hold values from 83886.08 to 1342177.2
- time_weight: float32 [128, 256], replicated, may hold values from -0.5 to 0.5
- time_moment: float32 [128, 256], replicated, may hold values from -2560 to 2560
- time_square: float32 [128, 256], replicated, may hold values from 83886.08 to 1342177.2
- vec_params: float32 [9, 128], replicated, may hold values from 0.5 to 1.5
- vec_moment: float32 [9, 128], replicated, may hold values from -4096 to 4096
- vec_square: float32 [9, 128], replicated, may hold values from 256901.12 to 4110418
Outputs:
- block_out: float32 [256, 128, 4096], P('wide', 'grp')
- field_grad: float32 [256, 8, 4096], P('wide', None, 'grp')
- in_new: float32 [72, 128], replicated
- in_first: float32 [72, 128], replicated
- in_second: float32 [72, 128], replicated
- in_low: bfloat16 [72, 128], replicated
- mid_new: float32 [2304, 128], P(('wide', 'grp'))
- mid_first: float32 [2304, 128], P(('wide', 'grp'))
- mid_second: float32 [2304, 128], P(('wide', 'grp'))
- mid_low: bfloat16 [2304, 128], P(('wide', 'grp'))
- time_new: float32 [128, 256], replicated
- time_first: float32 [128, 256], replicated
- time_second: float32 [128, 256], replicated
- vec_new: float32 [9, 128], replicated
- vec_first: float32 [9, 128], replicated
- vec_second: float32 [9, 128], replicated
All inputs are finite; a program needn't handle non-finite values. No bound on the sum of `slot_mask` on one device may be relied on, other than what follows from the above.
Results may differ from a plain program's by a relative error of at most 0.007.
Values may be sent and summed in bfloat16 or wider, within the bound.
No kernel may reach another device: no remote copies, remote signals or barrier semaphores. Data moves between devices by JAX's collectives and lax.ppermute only.
A program may use at most 512 MiB of HBM per device.

v0:
```python
import math

import jax
import jax.numpy as jnp
from jax import lax
from jax.sharding import PartitionSpec as P

C = 128
W = 64
TAPS = 9
GROUPS = 8
STEP = 4


highest = lax.Precision.HIGHEST
beta_one = 0.5
beta_two = 0.5
epsilon = 1e-08
weight_decay = 0.01
rate_in = 0.1
rate_mid = 0.03
rate_time = 0.1
rate_vecs = 0.3
norm_epsilon = 1e-05


def with_halo(x, sides, width):
    for axis, dim in sides:
        count, length = (lax.axis_size(axis), x.shape[dim])
        up = [(i, (i + 1) % count) for i in range(count)]
        down = [(j, i) for i, j in up]
        last = lax.slice_in_dim(x, length - width, length, axis=dim)
        first = lax.slice_in_dim(x, 0, width, axis=dim)
        before = lax.ppermute(last, axis, up)
        after = lax.ppermute(first, axis, down)
        x = jnp.concatenate([before, x, after], axis=dim)
    return x


def fourier(noise_step, feature_count):
    half_count = feature_count // 2
    frequency = jnp.exp(-math.log(10000.0) * jnp.arange(half_count, dtype=jnp.float32) / half_count)
    angles = noise_step.astype(jnp.float32)[:, None] * frequency[None, :]
    return jnp.concatenate([jnp.sin(angles), jnp.cos(angles)], axis=1)


def group_norm(values, gain_vec, beta_vec, group_width):
    item_count, chans, cells = values.shape
    grouped = values.reshape(item_count, chans // group_width, group_width * cells)
    group_mean = jnp.mean(grouped, axis=2, keepdims=True)
    centered = grouped - group_mean
    group_var = jnp.mean(centered * centered, axis=2, keepdims=True)
    normed = (centered * lax.rsqrt(group_var + norm_epsilon)).reshape(item_count, chans, cells)
    return normed * gain_vec[None, :, None] + beta_vec[None, :, None]


def adam_update(weight, grad, moment, square, rate, step_float):
    moment_new = beta_one * moment + (1.0 - beta_one) * grad
    square_new = beta_two * square + (1.0 - beta_two) * grad * grad
    moment_hat = moment_new / (1.0 - jnp.power(beta_one, step_float))
    square_hat = square_new / (1.0 - jnp.power(beta_two, step_float))
    weight_new = weight - rate * (
        moment_hat / (jnp.sqrt(square_hat) + epsilon) + weight_decay * weight
    )
    return (weight_new, moment_new, square_new)


def to_rows(values):
    return lax.all_to_all(values, "grp", split_axis=2, concat_axis=1, tiled=True)


def to_channels(values):
    return lax.all_to_all(values, "grp", split_axis=1, concat_axis=2, tiled=True)


def pad_strip(values):
    return with_halo(values, (("grp", 2),), W)


def conv_rows(padded, taps, strip_rows, row_width):
    item_count, chans = (padded.shape[0], padded.shape[1])
    grid_view = padded.reshape(item_count, chans, strip_rows + 2, row_width)
    running = jnp.zeros((item_count, taps.shape[2], strip_rows * row_width), jnp.float32)
    for row_shift in range(3):
        band_rows = grid_view[:, :, row_shift : row_shift + strip_rows, :]
        for col_shift in range(3):
            shifted = jnp.roll(band_rows, 1 - col_shift, axis=3).reshape(
                item_count, chans, strip_rows * row_width
            )
            running = running + jnp.einsum(
                "bcp,cd->bdp",
                shifted,
                taps[row_shift * 3 + col_shift],
                preferred_element_type=jnp.float32,
            )
    return running


def conv_adjoint(padded, taps, strip_rows, row_width):
    item_count, chans = (padded.shape[0], padded.shape[1])
    grid_view = padded.reshape(item_count, chans, strip_rows + 2, row_width)
    running = jnp.zeros((item_count, taps.shape[1], strip_rows * row_width), jnp.float32)
    for row_shift in range(3):
        band_rows = grid_view[:, :, 2 - row_shift : 2 - row_shift + strip_rows, :]
        for col_shift in range(3):
            shifted = jnp.roll(band_rows, col_shift - 1, axis=3).reshape(
                item_count, chans, strip_rows * row_width
            )
            running = running + jnp.einsum(
                "bdp,cd->bcp",
                shifted,
                taps[row_shift * 3 + col_shift],
                preferred_element_type=jnp.float32,
            )
    return running


def conv_weight_grad(padded, grads, strip_rows, row_width):
    item_count, chans = (padded.shape[0], padded.shape[1])
    grid_view = padded.reshape(item_count, chans, strip_rows + 2, row_width)
    pieces = []
    for row_shift in range(3):
        band_rows = grid_view[:, :, row_shift : row_shift + strip_rows, :]
        for col_shift in range(3):
            shifted = jnp.roll(band_rows, 1 - col_shift, axis=3).reshape(
                item_count, chans, strip_rows * row_width
            )
            pieces.append(
                jnp.einsum("bcp,bdp->cd", shifted, grads, preferred_element_type=jnp.float32)
            )
    return jnp.stack(pieces)


def local(
    fields,
    slot_mask,
    noise_step,
    cotangent,
    in_weight,
    in_moment,
    in_square,
    mid_weight,
    mid_moment,
    mid_square,
    time_weight,
    time_moment,
    time_square,
    vec_params,
    vec_moment,
    vec_square,
):
    row_width = W
    slot_count = fields.shape[1]
    strip_rows = fields.shape[2] // row_width
    own_chans = cotangent.shape[1]
    chans = own_chans * lax.axis_size("grp")
    group_width = C // GROUPS
    chan_start = lax.axis_index("grp") * own_chans
    gathered = lax.all_gather(mid_weight.astype(jnp.bfloat16), ("wide", "grp"), axis=0, tiled=True)
    inner_taps = gathered.reshape(2, TAPS, chans, chans)
    input_taps = in_weight.astype(jnp.bfloat16).reshape(TAPS, slot_count, chans)
    features = fourier(noise_step, time_weight.shape[0])
    vec_own = lax.dynamic_slice_in_dim(vec_params, chan_start, own_chans, 1)
    mask_float = slot_mask.astype(jnp.float32)[:, :, None]
    masked_low = (fields * mask_float).astype(jnp.bfloat16)
    masked_padded = with_halo(masked_low, (("grp", 2),), row_width)
    lifted_bf = conv_rows(masked_padded, input_taps, strip_rows, row_width).astype(jnp.bfloat16)
    lifted = to_channels(lifted_bf).astype(jnp.float32)

    def first_section(lifted_val, bias_in, gain_one, beta_first):
        return jax.nn.gelu(
            group_norm(lifted_val + bias_in[None, :, None], gain_one, beta_first, group_width)
        )

    first_act, first_pullback = jax.vjp(first_section, lifted, vec_own[0], vec_own[1], vec_own[2])
    first_padded = pad_strip(to_rows(first_act.astype(jnp.bfloat16)))
    first_conv = conv_rows(first_padded, inner_taps[0], strip_rows, row_width).astype(jnp.bfloat16)
    first_out = to_channels(first_conv).astype(jnp.float32)
    scale_cols = lax.dynamic_slice_in_dim(time_weight, chan_start, own_chans, 1)
    offset_cols = lax.dynamic_slice_in_dim(time_weight, chans + chan_start, own_chans, 1)

    def second_section(
        conv_val,
        bias_mid,
        weight_scale,
        weight_offset,
        bias_scale,
        bias_offset,
        gain_two,
        beta_second,
    ):
        scaling = jnp.dot(features, weight_scale, precision=highest) + bias_scale[None, :]
        offset = jnp.dot(features, weight_offset, precision=highest) + bias_offset[None, :]
        modulated = (conv_val + bias_mid[None, :, None]) * (1.0 + scaling[:, :, None]) + offset[
            :, :, None
        ]
        return jax.nn.gelu(group_norm(modulated, gain_two, beta_second, group_width))

    second_act, second_pullback = jax.vjp(
        second_section,
        first_out,
        vec_own[3],
        scale_cols,
        offset_cols,
        vec_own[4],
        vec_own[5],
        vec_own[6],
        vec_own[7],
    )
    second_padded = pad_strip(to_rows(second_act.astype(jnp.bfloat16)))
    second_bf = conv_rows(second_padded, inner_taps[1], strip_rows, row_width).astype(jnp.bfloat16)
    second_out = to_channels(second_bf).astype(jnp.float32)
    block_out = lifted + vec_own[0][None, :, None] + second_out + vec_own[8][None, :, None]
    out_rows = to_rows(cotangent)
    grad_second = conv_weight_grad(second_padded, out_rows, strip_rows, row_width)
    d_second = conv_adjoint(pad_strip(out_rows), inner_taps[1], strip_rows, row_width).astype(
        jnp.bfloat16
    )
    vec_grad = jnp.zeros((9, chans), jnp.float32)
    time_grad = jnp.zeros((time_weight.shape[0], 2 * chans), jnp.float32)
    d_second_act = to_channels(d_second).astype(jnp.float32)
    d_conv, d_bias_mid, d_wscale, d_woffset, d_bscale, d_boffset, d_gain_two, d_beta_second = (
        second_pullback(d_second_act)
    )
    d_first_rows = to_rows(d_conv.astype(jnp.bfloat16))
    middle_vecs = jnp.stack([d_bias_mid, d_bscale, d_boffset, d_gain_two, d_beta_second])
    vec_grad = lax.dynamic_update_slice(vec_grad, middle_vecs, (jnp.int32(3), chan_start))
    time_grad = lax.dynamic_update_slice(time_grad, d_wscale, (jnp.int32(0), chan_start))
    time_grad = lax.dynamic_update_slice(time_grad, d_woffset, (jnp.int32(0), chans + chan_start))
    grad_first = conv_weight_grad(first_padded, d_first_rows, strip_rows, row_width)
    d_first_bf = conv_adjoint(pad_strip(d_first_rows), inner_taps[0], strip_rows, row_width).astype(
        jnp.bfloat16
    )
    out_grad = cotangent.astype(jnp.float32)
    d_first_act = to_channels(d_first_bf).astype(jnp.float32)
    d_lifted_branch, d_bias_in, d_gain_one, d_beta_first = first_pullback(d_first_act)
    d_hidden = out_grad + d_lifted_branch
    out_sum = jnp.sum(out_grad, axis=(0, 2))
    outer_vecs = jnp.stack([d_bias_in + out_sum, d_gain_one, d_beta_first])
    vec_grad = lax.dynamic_update_slice(vec_grad, outer_vecs, (jnp.int32(0), chan_start))
    vec_grad = lax.dynamic_update_slice(vec_grad, out_sum[None, :], (jnp.int32(8), chan_start))
    lifted_rows = to_rows(d_hidden.astype(jnp.bfloat16))
    grad_in = conv_weight_grad(masked_padded, lifted_rows, strip_rows, row_width).reshape(
        TAPS * slot_count, chans
    )
    field_grad = (
        conv_adjoint(pad_strip(lifted_rows), input_taps, strip_rows, row_width) * mask_float
    )
    mid_grad = jnp.concatenate(
        [grad_first.reshape(TAPS * chans, chans), grad_second.reshape(TAPS * chans, chans)], axis=0
    )
    share_rows = mid_weight.shape[0]
    mid_total, in_total, time_total, vec_total = lax.psum(
        (mid_grad, grad_in, time_grad, vec_grad), ("wide", "grp")
    )
    mid_total = lax.dynamic_slice_in_dim(
        mid_total, lax.axis_index(("wide", "grp")) * share_rows, share_rows, 0
    )
    step_float = jnp.float32(STEP)
    in_new, in_first, in_second = adam_update(
        in_weight, in_total, in_moment, in_square, rate_in, step_float
    )
    mid_new, mid_first, mid_second = adam_update(
        mid_weight, mid_total, mid_moment, mid_square, rate_mid, step_float
    )
    time_new, time_first, time_second = adam_update(
        time_weight, time_total, time_moment, time_square, rate_time, step_float
    )
    vec_new, vec_first, vec_second = adam_update(
        vec_params, vec_total, vec_moment, vec_square, rate_vecs, step_float
    )
    return (
        block_out,
        field_grad,
        in_new,
        in_first,
        in_second,
        in_new.astype(jnp.bfloat16),
        mid_new,
        mid_first,
        mid_second,
        mid_new.astype(jnp.bfloat16),
        time_new,
        time_first,
        time_second,
        vec_new,
        vec_first,
        vec_second,
    )


def solution(mesh):
    return jax.shard_map(
        local,
        mesh=mesh,
        in_specs=(
            P("wide", None, "grp"),
            P("wide", None),
            P("wide"),
            P("wide", "grp", None),
            P(),
            P(),
            P(),
            P(("wide", "grp"), None),
            P(("wide", "grp"), None),
            P(("wide", "grp"), None),
            P(),
            P(),
            P(),
            P(),
            P(),
            P(),
        ),
        out_specs=(
            P("wide", "grp", None),
            P("wide", None, "grp"),
            P(),
            P(),
            P(),
            P(),
            P(("wide", "grp"), None),
            P(("wide", "grp"), None),
            P(("wide", "grp"), None),
            P(("wide", "grp"), None),
            P(),
            P(),
            P(),
            P(),
            P(),
            P(),
        ),
        check_vma=False,
    )
```

profile of v0, /device:TPU:0, one launch (start us, length us, event | category | flops | bytes accessed | tf_op | source)
XLA Modules:
  0.0 3005.5 jit_solution(1742158889226896423)
XLA Ops:
  32.8 23.8 reshape.882
  156.5 44.3 %fusion.72 = bf16[16,128,2048]{1,2,0:T(8,128)(2,1)} fusion(f32[16,2048,128]{2,1,0:T(8,128)} %fusion.155, f32[16,2048,128]{2,1,0:T(8,128)} %fusion.154, f32[16,2048,128]{2,1,0:T(8,128)} %fusion.153, f32[16,2048,128]{2,1,0:T(8,128)} %fusion.152, f32[16,2048,128]{2,1,0:T(8,128)} %fusion.151, f32[16,2048,128]{2,1,0:T(8,128)} %fusion.150, ...), kind=kOutput, calls=%fused_computation.112 | convolution fusion | flops 104857600 | bytes 143132672 | tf_op jit(solution)/shard_map/bcp,cd->bdp/dot_general | solution.py:90
  221.0 154.5 %all_gather.3 = bf16[2304,128]{1,0:T(8,128)(2,1)S(1)} all-gather(bf16[72,128]{1,0:T(8,128)(2,1)S(1)} %convert_element_type.192), channel_id=1, replica_groups=mesh['wide'=16,'grp'=2] {'wide','grp'}, dimensions={0}, use_global_device_ids=true | all-gather | bytes 608256 | tf_op jit(solution)/shard_map/all_gather | solution.py:159
  375.5 23.9 reshape.883
  489.0 24.0 reshape.878
  548.8 36.6 %fusion.172 = (bf16[16,128,32,63]{1,3,2,0:T(8,128)(2,1)}, bf16[16,128,32,63]{1,3,2,0:T(8,128)(2,1)}, bf16[16,128,32,63]{1,3,2,0:T(8,128)(2,1)}, bf16[16,128,32,6...) fusion(bf16[16,128,34,64]{1,3,2,0:T(8,128)(2,1)} %bitcast.700), kind=kLoop, calls=%fused_computation.345 | loop fusion | bytes 99090432 | tf_op jit(solution)/shard_map/jit(_roll_static)/slice | solution.py:106
  692.5 23.6 reshape.879
  716.1 27.3 copy.457
  757.7 46.6 %fusion.75 = bf16[16,128,2048]{1,2,0:T(8,128)(2,1)} fusion(f32[16,2048,128]{2,1,0:T(8,128)} %fusion.142, f32[16,2048,128]{2,1,0:T(8,128)} %fusion.140, f32[16,2048,128]{2,1,0:T(8,128)} %fusion.138, f32[16,2048,128]{2,1,0:T(8,128)} %fusion.136, f32[16,2048,128]{2,1,0:T(8,128)} %fusion.134, f32[16,2048,128]{2,1,0:T(8,128)} %fusion.132, ...), kind=kOutput, calls=%fused_computation.115 | convolution fusion | flops 1111490560 | bytes 151027712 | tf_op jit(solution)/shard_map/bdp,cd->bcp/dot_general | solution.py:109
  852.6 35.7 %fusion.177 = (bf16[16,128,32,63]{1,3,2,0:T(8,128)(2,1)}, bf16[16,128,32,63]{1,3,2,0:T(8,128)(2,1)}, bf16[16,128,32,63]{1,3,2,0:T(8,128)(2,1)}, bf16[16,128,32,6...) fusion(bf16[16,128,34,64]{1,3,2,0:T(8,128)(2,1)} %bitcast.708), kind=kLoop, calls=%fused_computation.350 | loop fusion | bytes 99090432 | tf_op jit(solution)/shard_map/jit(_roll_static)/slice | solution.py:87
  1057.7 46.8 %fusion.73 = bf16[16,128,2048]{1,2,0:T(8,128)(2,1)} fusion(f32[16,2048,128]{2,1,0:T(8,128)} %fusion.127, f32[16,2048,128]{2,1,0:T(8,128)} %fusion.125, f32[16,2048,128]{2,1,0:T(8,128)} %fusion.123, f32[16,2048,128]{2,1,0:T(8,128)} %fusion.121, f32[16,2048,128]{2,1,0:T(8,128)} %fusion.119, f32[16,2048,128]{2,1,0:T(8,128)} %fusion.117, ...), kind=kOutput, calls=%fused_computation.113 | convolution fusion | flops 1111490560 | bytes 151027712 | tf_op jit(solution)/shard_map/bcp,cd->bdp/dot_general | solution.py:90
  1159.7 53.1 %all-to-all-done.2 = bf16[16,128,2048]{2,0,1:T(8,128)(2,1)} async-done(((bf16[16,128,2048]{2,0,1:T(8,128)(2,1)}), bf16[16,128,2048]{2,0,1:T(8,128)(2,1)}, u32[]{:S(2)}, u32[]{:S(2)}) %all-to-all-start.2) | async-done | bytes 8388640 | tf_op jit(solution)/shard_map/all_to_all | solution.py:73
  1238.8 20.9 fusion.33
  1268.6 25.4 add_add_fusion.2
  1307.4 24.8 fusion.66
  1352.5 23.8 reshape.884
  1403.7 23.7 reshape.880
  1442.5 28.6 all-to-all-done.7
  1478.1 24.0 reshape.885
  1572.0 23.8 reshape.881
  1595.7 27.3 copy.458
  1689.6 36.2 %fusion.174 = (bf16[16,128,32,63]{1,3,2,0:T(8,128)(2,1)}, bf16[16,128,32,63]{1,3,2,0:T(8,128)(2,1)}, bf16[16,128,32,63]{1,3,2,0:T(8,128)(2,1)}, bf16[16,128,32,6...) fusion(bf16[16,128,34,64]{1,3,2,0:T(8,128)(2,1)} %bitcast.711), kind=kLoop, calls=%fused_computation.347 | loop fusion | bytes 99090432 | tf_op jit(solution)/shard_map/jit(_roll_static)/slice | solution.py:87
  1777.5 36.9 %fusion.169 = (bf16[16,128,32,63]{1,3,2,0:T(8,128)(2,1)}, bf16[16,128,32,63]{1,3,2,0:T(8,128)(2,1)}, bf16[16,128,32,63]{1,3,2,0:T(8,128)(2,1)}, bf16[16,128,32,6...) fusion(bf16[16,128,34,64]{1,3,2,0:T(8,128)(2,1)} %bitcast.705), kind=kLoop, calls=%fused_computation.342 | loop fusion | bytes 99090432 | tf_op jit(solution)/shard_map/jit(_roll_static)/slice | solution.py:106
  2020.5 46.7 %fusion.76 = bf16[16,128,2048]{1,2,0:T(8,128)(2,1)} fusion(f32[16,2048,128]{2,1,0:T(8,128)} %fusion.126, f32[16,2048,128]{2,1,0:T(8,128)} %fusion.124, f32[16,2048,128]{2,1,0:T(8,128)} %fusion.122, f32[16,2048,128]{2,1,0:T(8,128)} %fusion.120, f32[16,2048,128]{2,1,0:T(8,128)} %fusion.118, f32[16,2048,128]{2,1,0:T(8,128)} %fusion.116, ...), kind=kOutput, calls=%fused_computation.116 | convolution fusion | flops 1111490560 | bytes 151027712 | tf_op jit(solution)/shard_map/bdp,cd->bcp/dot_general | solution.py:109
  2204.3 46.7 %fusion.74 = bf16[16,128,2048]{1,2,0:T(8,128)(2,1)} fusion(f32[16,2048,128]{2,1,0:T(8,128)} %fusion.143, f32[16,2048,128]{2,1,0:T(8,128)} %fusion.141, f32[16,2048,128]{2,1,0:T(8,128)} %fusion.139, f32[16,2048,128]{2,1,0:T(8,128)} %fusion.137, f32[16,2048,128]{2,1,0:T(8,128)} %fusion.135, f32[16,2048,128]{2,1,0:T(8,128)} %fusion.133, ...), kind=kOutput, calls=%fused_computation.114 | convolution fusion | flops 1111490560 | bytes 151027712 | tf_op jit(solution)/shard_map/bcp,cd->bdp/dot_general | solution.py:90
  2342.9 23.7 add_add_fusion
  2432.5 31.9 %fusion.4 = (bf16[16,64,4096]{2,1,0:T(8,128)(2,1)}, f32[16,64,4096]{2,1,0:T(8,128)}, f32[64]{0:T(128)S(1)}) fusion(bf16[16,64,4096]{2,1,0:T(8,128)(2,1)S(1)} %bitcast.852, f32[16,64,4096]{2,1,0:T(8,128)} %bitcast.790, f32[16,64,4096]{2,1,0:T(8,128)} %bitcast.776, f32[16,64]{1,0:T(8,128)S(1)} %broadcast_in_dim.64, f32[16,64]{1,0:T(8,128)S(1)} %broadcast_in_dim.60, ...), kind=kLoop, calls=%fused_computation.26 | loop fusion | flops 150994880 | bytes 83903744 | tf_op jit(solution)/shard_map/convert_element_type | solution.py:242
  2484.7 23.9 reshape.886
  2535.2 142.7 %all-reduce.4.cloned.1.call-done = (f32[2304,128]{1,0:T(8,128)}, f32[128,256]{1,0:T(8,128)}) async-done(((f32[2304,128]{1,0:T(8,128)}, f32[128,256]{1,0:T(8,128)}), (f32[2304,128]{1,0:T(8,128)}, f32[128,256]{1,0:T(8,128)})) %all-reduce.4.cloned.1.call-update) | async-done | bytes 1310736 | tf_op jit(solution)/shard_map/psum | solution.py:253
  2689.7 23.4 reshape.887
  2763.4 54.8 %all-reduce = (f32[72,128]{1,0:T(8,128)S(1)}, f32[9,128]{1,0:T(8,128)S(1)}) all-reduce(f32[72,128]{1,0:T(8,128)S(1)} %bitcast.861, f32[9,128]{1,0:T(8,128)S(1)} %dynamic_update_slice.19), channel_id=1, replica_groups=mesh['wide'=16,'grp'=2] {'wide','grp'}, use_global_device_ids=true, to_apply=%region_16.17 | all-reduce | flops 10368 | bytes 82944 | tf_op jit(solution)/shard_map/psum | solution.py:253
  2847.9 36.4 %fusion.166 = (bf16[16,128,32,63]{1,3,2,0:T(8,128)(2,1)}, bf16[16,128,32,63]{1,3,2,0:T(8,128)(2,1)}, bf16[16,128,32,63]{1,3,2,0:T(8,128)(2,1)}, bf16[16,128,32,6...) fusion(bf16[16,128,34,64]{1,3,2,0:T(8,128)(2,1)} %bitcast.714), kind=kLoop, calls=%fused_computation.339 | loop fusion | bytes 99090432 | tf_op jit(solution)/shard_map/jit(_roll_static)/slice | solution.py:106
  (626 shorter events, 1723.6 us)
Async XLA Ops:
  9.4 54.6 %collective-permute-start = (bf16[16,8,64]{2,1,0:T(8,128)(2,1)S(1)}, bf16[16,8,64]{2,1,0:T(8,128)(2,1)S(1)}, u32[]{:S(2)}, u32[]{:S(2)}) collective-permute-start(bf16[16,8,64]{2,1,0:T(8,128)(2,1)S(1)} %get-tuple-element.155), channel_id=1, source_target_pairs={{0,1},{1,0},{2,3},{3,2},{4,5},{5,4},{6,7},{7,6},{8,9},{9,8},{10,11... | collective-permute-start | bytes 49160 | tf_op jit(solution)/shard_map/ppermute | solution.py:34
  12.4 51.6 %collective-permute-start.1 = (bf16[16,8,64]{2,1,0:T(8,128)(2,1)S(1)}, bf16[16,8,64]{2,1,0:T(8,128)(2,1)S(1)}, u32[]{:S(2)}, u32[]{:S(2)}) collective-permute-start(bf16[16,8,64]{2,1,0:T(8,128)(2,1)S(1)} %get-tuple-element.154), channel_id=1, source_target_pairs={{1,0},{0,1},{3,2},{2,3},{5,4},{4,5},{7,6},{6,7},{9,8},{8,9},{11,10... | collective-permute-start | bytes 49160 | tf_op jit(solution)/shard_map/ppermute | solution.py:35
  56.6 156.8 %all-to-all-start.5 = ((bf16[2,2,1048576]{2,1,0:T(2,128)(2,1)}), bf16[2,2,1048576]{2,1,0:T(2,128)(2,1)}, u32[]{:S(2)}, u32[]{:S(2)}) async-start(bf16[2,2,1048576]{2,1,0:T(2,128)(2,1)} %reshape.882), calls=%async_computation.5 | async-start | bytes 16777216 | tf_op jit(solution)/shard_map/all_to_all | solution.py:69
  213.3 208.0 %all-to-all-start = ((bf16[16,128,2048]{2,0,1:T(8,128)(2,1)}), bf16[16,128,2048]{2,0,1:T(8,128)(2,1)}, u32[]{:S(2)}, u32[]{:S(2)}) async-start(bf16[16,128,2048]{2,0,1:T(8,128)(2,1)} %copy.350), calls=%async_computation | async-start | bytes 16777216 | tf_op jit(solution)/shard_map/all_to_all | solution.py:73
  221.0 232.0 %copy-start.68 = (f32[64]{0:T(128)}, f32[64]{0:T(128)S(1)}, u32[]{:S(2)}) copy-start(f32[64]{0:T(128)S(1)} %get-tuple-element.163) | copy-start | bytes 772
  221.0 232.0 %copy-start.72 = (f32[64]{0:T(128)}, f32[64]{0:T(128)S(1)}, u32[]{:S(2)}) copy-start(f32[64]{0:T(128)S(1)} %get-tuple-element.162) | copy-start | bytes 772
  221.0 232.0 %copy-start.76 = (f32[64]{0:T(128)}, f32[64]{0:T(128)S(1)}, u32[]{:S(2)}) copy-start(f32[64]{0:T(128)S(1)} %get-tuple-element.161) | copy-start | bytes 772
  375.5 682.2 %copy-start.5 = (bf16[2304,128]{1,0:T(8,128)(2,1)}, bf16[2304,128]{1,0:T(8,128)(2,1)S(1)}, u32[]{:S(2)}) copy-start(bf16[2304,128]{1,0:T(8,128)(2,1)S(1)} %all_gather.3) | copy-start | bytes 1769476
  419.2 100.8 %collective-permute-start.6 = (bf16[16,128,64]{2,1,0:T(8,128)(2,1)S(1)}, bf16[16,128,64]{2,1,0:T(8,128)(2,1)S(1)}, u32[]{:S(2)}, u32[]{:S(2)}) collective-permute-start(bf16[16,128,64]{2,1,0:T(8,128)(2,1)S(1)} %get-tuple-element.130), channel_id=1, source_target_pairs={{0,1},{1,0},{2,3},{3,2},{4,5},{5,4},{6,7},{7,6},{8,9},{9,8},{10,11... | collective-permute-start | bytes 786440 | tf_op jit(solution)/shard_map/ppermute | solution.py:34
  419.3 100.7 %collective-permute-start.7 = (bf16[16,128,64]{2,1,0:T(8,128)(2,1)S(1)}, bf16[16,128,64]{2,1,0:T(8,128)(2,1)S(1)}, u32[]{:S(2)}, u32[]{:S(2)}) collective-permute-start(bf16[16,128,64]{2,1,0:T(8,128)(2,1)S(1)} %get-tuple-element.129), channel_id=1, source_target_pairs={{1,0},{0,1},{3,2},{2,3},{5,4},{4,5},{7,6},{6,7},{9,8},{8,9},{11,10... | collective-permute-start | bytes 786440 | tf_op jit(solution)/shard_map/ppermute | solution.py:35
  513.0 179.5 %all-to-all-start.1 = ((bf16[2,2,1048576]{2,1,0:T(2,128)(2,1)}), bf16[2,2,1048576]{2,1,0:T(2,128)(2,1)}, u32[]{:S(2)}, u32[]{:S(2)}) async-start(bf16[2,2,1048576]{2,1,0:T(2,128)(2,1)} %reshape.878), calls=%async_computation.1 | async-start | bytes 16777216 | tf_op jit(solution)/shard_map/all_to_all | solution.py:69
  755.6 68.2 %collective-permute-start.2 = (bf16[16,128,64]{2,1,0:T(8,128)(2,1)S(1)}, bf16[16,128,64]{2,1,0:T(8,128)(2,1)S(1)}, u32[]{:S(2)}, u32[]{:S(2)}) collective-permute-start(bf16[16,128,64]{2,1,0:T(8,128)(2,1)S(1)} %get-tuple-element.136), channel_id=1, source_target_pairs={{0,1},{1,0},{2,3},{3,2},{4,5},{5,4},{6,7},{7,6},{8,9},{9,8},{10,11... | collective-permute-start | bytes 786440 | tf_op jit(solution)/shard_map/ppermute | solution.py:34
  757.7 66.2 %collective-permute-start.3 = (bf16[16,128,64]{2,1,0:T(8,128)(2,1)S(1)}, bf16[16,128,64]{2,1,0:T(8,128)(2,1)S(1)}, u32[]{:S(2)}, u32[]{:S(2)}) collective-permute-start(bf16[16,128,64]{2,1,0:T(8,128)(2,1)S(1)} %get-tuple-element.135), channel_id=1, source_target_pairs={{1,0},{0,1},{3,2},{2,3},{5,4},{4,5},{7,6},{6,7},{9,8},{8,9},{11,10... | collective-permute-start | bytes 786440 | tf_op jit(solution)/shard_map/ppermute | solution.py:35
  816.9 300.3 %all-to-all-start.6 = ((bf16[16,128,2048]{2,0,1:T(8,128)(2,1)}), bf16[16,128,2048]{2,0,1:T(8,128)(2,1)}, u32[]{:S(2)}, u32[]{:S(2)}) async-start(bf16[16,128,2048]{2,0,1:T(8,128)(2,1)} %copy.378), calls=%async_computation.6 | async-start | bytes 16777216 | tf_op jit(solution)/shard_map/all_to_all | solution.py:73
  1117.1 95.7 %all-to-all-start.2 = ((bf16[16,128,2048]{2,0,1:T(8,128)(2,1)}), bf16[16,128,2048]{2,0,1:T(8,128)(2,1)}, u32[]{:S(2)}, u32[]{:S(2)}) async-start(bf16[16,128,2048]{2,0,1:T(8,128)(2,1)} %copy.361), calls=%async_computation.2 | async-start | bytes 16777216 | tf_op jit(solution)/shard_map/all_to_all | solution.py:73
  1376.3 94.8 %all-to-all-start.7 = ((bf16[2,2,1048576]{2,1,0:T(2,128)(2,1)}), bf16[2,2,1048576]{2,1,0:T(2,128)(2,1)}, u32[]{:S(2)}, u32[]{:S(2)}) async-start(bf16[2,2,1048576]{2,1,0:T(2,128)(2,1)} %reshape.884), calls=%async_computation.7 | async-start | bytes 16777216 | tf_op jit(solution)/shard_map/all_to_all | solution.py:69
  1471.1 100.9 %all-to-all-start.3 = ((bf16[2,2,1048576]{2,1,0:T(2,128)(2,1)}), bf16[2,2,1048576]{2,1,0:T(2,128)(2,1)}, u32[]{:S(2)}, u32[]{:S(2)}) async-start(bf16[2,2,1048576]{2,1,0:T(2,128)(2,1)} %reshape.880), calls=%async_computation.3 | async-start | bytes 16777216 | tf_op jit(solution)/shard_map/all_to_all | solution.py:69
  1635.1 14.9 collective-permute-start.4
  1637.1 24.1 collective-permute-start.5
  1638.6 110.5 %collective-permute-start.8 = (bf16[16,128,64]{2,1,0:T(8,128)(2,1)S(1)}, bf16[16,128,64]{2,1,0:T(8,128)(2,1)S(1)}, u32[]{:S(2)}, u32[]{:S(2)}) collective-permute-start(bf16[16,128,64]{2,1,0:T(8,128)(2,1)S(1)} %get-tuple-element.128), channel_id=1, source_target_pairs={{0,1},{1,0},{2,3},{3,2},{4,5},{5,4},{6,7},{7,6},{8,9},{9,8},{10,11... | collective-permute-start | bytes 786440 | tf_op jit(solution)/shard_map/ppermute | solution.py:34
  1640.6 108.5 %collective-permute-start.9 = (bf16[16,128,64]{2,1,0:T(8,128)(2,1)S(1)}, bf16[16,128,64]{2,1,0:T(8,128)(2,1)S(1)}, u32[]{:S(2)}, u32[]{:S(2)}) collective-permute-start(bf16[16,128,64]{2,1,0:T(8,128)(2,1)S(1)} %get-tuple-element.127), channel_id=1, source_target_pairs={{1,0},{0,1},{3,2},{2,3},{5,4},{4,5},{7,6},{6,7},{9,8},{8,9},{11,10... | collective-permute-start | bytes 786440 | tf_op jit(solution)/shard_map/ppermute | solution.py:35
  2079.8 217.6 %all-to-all-start.8 = ((bf16[16,128,2048]{2,0,1:T(8,128)(2,1)}), bf16[16,128,2048]{2,0,1:T(8,128)(2,1)}, u32[]{:S(2)}, u32[]{:S(2)}) async-start(bf16[16,128,2048]{2,0,1:T(8,128)(2,1)} %copy.388), calls=%async_computation.8 | async-start | bytes 16777216 | tf_op jit(solution)/shard_map/all_to_all | solution.py:73
  2297.4 87.9 %all-to-all-start.4 = ((bf16[16,128,2048]{2,0,1:T(8,128)(2,1)}), bf16[16,128,2048]{2,0,1:T(8,128)(2,1)}, u32[]{:S(2)}, u32[]{:S(2)}) async-start(bf16[16,128,2048]{2,0,1:T(8,128)(2,1)} %copy.372), calls=%async_computation.4 | async-start | bytes 16777216 | tf_op jit(solution)/shard_map/all_to_all | solution.py:73
  2508.6 181.0 %all-to-all-start.9 = ((bf16[2,2,1048576]{2,1,0:T(2,128)(2,1)}), bf16[2,2,1048576]{2,1,0:T(2,128)(2,1)}, u32[]{:S(2)}, u32[]{:S(2)}) async-start(bf16[2,2,1048576]{2,1,0:T(2,128)(2,1)} %reshape.886), calls=%async_computation.9 | async-start | bytes 16777216 | tf_op jit(solution)/shard_map/all_to_all | solution.py:69
  2515.6 162.3 %all-reduce.4.cloned.1.call-start = ((), (), s32[]{:S(2)}) async-start(), calls=%async_computation.10 | async-start | bytes 2621440 | tf_op jit(solution)/shard_map/psum | solution.py:253
  2523.9 154.0 %copy-start.58 = (f32[72,128]{1,0:T(8,128)S(1)}, f32[72,128]{1,0:T(8,128)}, u32[]{:S(2)}) copy-start(f32[72,128]{1,0:T(8,128)} %param.23) | copy-start | bytes 110596
  2523.9 154.0 %copy-start.63 = (f32[72,128]{1,0:T(8,128)S(1)}, f32[72,128]{1,0:T(8,128)}, u32[]{:S(2)}) copy-start(f32[72,128]{1,0:T(8,128)} %param.25) | copy-start | bytes 110596
  2523.9 155.4 %copy-start.47 = (f32[128,256]{1,0:T(8,128)S(1)}, f32[128,256]{1,0:T(8,128)}, u32[]{:S(2)}) copy-start(f32[128,256]{1,0:T(8,128)} %param.26) | copy-start | bytes 393220
  2523.9 155.4 %copy-start.61 = (f32[128,256]{1,0:T(8,128)S(1)}, f32[128,256]{1,0:T(8,128)}, u32[]{:S(2)}) copy-start(f32[128,256]{1,0:T(8,128)} %param.28) | copy-start | bytes 393220
  2524.0 155.4 %copy-start.62 = (f32[128,256]{1,0:T(8,128)S(1)}, f32[128,256]{1,0:T(8,128)}, u32[]{:S(2)}) copy-start(f32[128,256]{1,0:T(8,128)} %param.27) | copy-start | bytes 393220
  2761.3 58.2 %collective-permute-start.10 = (bf16[16,128,64]{2,1,0:T(8,128)(2,1)S(1)}, bf16[16,128,64]{2,1,0:T(8,128)(2,1)S(1)}, u32[]{:S(2)}, u32[]{:S(2)}) collective-permute-start(bf16[16,128,64]{2,1,0:T(8,128)(2,1)S(1)} %get-tuple-element.126), channel_id=1, source_target_pairs={{0,1},{1,0},{2,3},{3,2},{4,5},{5,4},{6,7},{7,6},{8,9},{9,8},{10,11... | collective-permute-start | bytes 786440 | tf_op jit(solution)/shard_map/ppermute | solution.py:34
  2763.1 56.4 %collective-permute-start.11 = (bf16[16,128,64]{2,1,0:T(8,128)(2,1)S(1)}, bf16[16,128,64]{2,1,0:T(8,128)(2,1)S(1)}, u32[]{:S(2)}, u32[]{:S(2)}) collective-permute-start(bf16[16,128,64]{2,1,0:T(8,128)(2,1)S(1)} %get-tuple-element.125), channel_id=1, source_target_pairs={{1,0},{0,1},{3,2},{2,3},{5,4},{4,5},{7,6},{6,7},{9,8},{8,9},{11,10... | collective-permute-start | bytes 786440 | tf_op jit(solution)/shard_map/ppermute | solution.py:35
  (137 other events, 2456.3 us)
Sparse Core Ops, SparseCore 0:
  2534.5 143.3 all-reduce.3
where the time goes:
time: 3020 us; the launch traced here: 3010 us
  local copies, waits for them, and re-layouts  1100 us (36%)
  matrix products  771 us (26%)
  other arithmetic  579 us (19%)
  waiting for transfers between devices  245 us (8%)
  blocking collectives  209 us (7%)
  starting transfers between devices  84.4 us (3%)
    dot_general x27, matrix products, conv_rows(): jnp.einsum('bcp,cd->bdp', shifted, taps[row_shift * 3 + col_shift], prefe...  364 us
    unnamed x307, local copies, waits for them, and re-layouts  273 us
    dot_general x27, matrix products, conv_adjoint(): jnp.einsum('bdp,cd->bcp', shifted, taps[row_shift * 3 + col_shift], prefe...  265 us
    concatenate x15, other arithmetic, conv_adjoint(): jnp.roll(band_rows, col_shift - 1, axis=3)  155 us
    all_gather x1, blocking collectives, local(): lax.all_gather(mid_weight.astype(jnp.bfloat16), ('wide', 'grp'), axis=0,...  154 us
    concatenate x11, local copies, waits for them, and re-layouts, with_halo(): x = jnp.concatenate([before, x, after], axis=dim)  143 us
    psum x1, waiting for transfers between devices, local(): lax.psum((mid_grad, grad_in, time_grad, vec_grad), ('wide', 'grp'))  143 us
    dot_general x27, matrix products, conv_weight_grad(): jnp.einsum('bcp,bdp->cd', shifted, grads, preferred_element_type=jnp.floa...  141 us
  transfers between devices with their start and end apart: 23, of which 5 were waited for; matrix products, arithmetic and copies ran while one was open for 48% of the time, Pallas kernels for 0%

commit v1 on v0

v1 whole, which is shorter than its diff:
```python
import functools
import math

import jax
import jax.numpy as jnp
from jax import lax
from jax.experimental import pallas as pl
from jax.experimental.pallas import tpu as pltpu
from jax.sharding import PartitionSpec as P

C = 128
W = 64
H = 64
PIX = H * W
TAPS = 9
GROUPS = 8
STEP = 4
NJ = 4
NS = W // NJ
ROWS = H * NS

highest = lax.Precision.HIGHEST
beta_one = 0.5
beta_two = 0.5
epsilon = 1e-08
weight_decay = 0.01
rate_in = 0.1
rate_mid = 0.03
rate_time = 0.1
rate_vecs = 0.3
norm_epsilon = 1e-05
bf = jnp.bfloat16
f32 = jnp.float32
GELU_C = math.sqrt(2.0 / math.pi)
GELU_K = 0.044715
VMEM_LIMIT = 58 << 20


def fourier(noise_step, feature_count):
    half_count = feature_count // 2
    frequency = jnp.exp(-math.log(10000.0) * jnp.arange(half_count, dtype=jnp.float32) / half_count)
    angles = noise_step.astype(jnp.float32)[:, None] * frequency[None, :]
    return jnp.concatenate([jnp.sin(angles), jnp.cos(angles)], axis=1)


def adam_update(weight, grad, moment, square, rate, step_float):
    moment_new = beta_one * moment + (1.0 - beta_one) * grad
    square_new = beta_two * square + (1.0 - beta_two) * grad * grad
    moment_hat = moment_new / (1.0 - jnp.power(beta_one, step_float))
    square_hat = square_new / (1.0 - jnp.power(beta_two, step_float))
    weight_new = weight - rate * (
        moment_hat / (jnp.sqrt(square_hat) + epsilon) + weight_decay * weight
    )
    return (weight_new, moment_new, square_new)


def group_sum(v):
    lane = lax.broadcasted_iota(jnp.int32, v.shape, 1)
    for k in (1, 2, 4, 8):
        v = v + jnp.where((lane & k) == 0, pltpu.roll(v, C - k, 1), pltpu.roll(v, k, 1))
    return v


def rows8(v):
    return jnp.sum(v.reshape(v.shape[0] // 8, 8, v.shape[1]), axis=0)


def gelu(x):
    x2 = x * x
    t = jnp.tanh(x * (GELU_C + (GELU_C * GELU_K) * x2))
    h = 0.5 * x
    return h + h * t


def gelu_slope(x):
    x2 = x * x
    t = jnp.tanh(x * (GELU_C + (GELU_C * GELU_K) * x2))
    q = (0.5 * GELU_C) + (1.5 * GELU_C * GELU_K) * x2
    return (0.5 + 0.5 * t) + (x * q) * (1.0 - t * t)


def band_weights(k_ref, t_ref, adjoint):
    zero = jnp.zeros((C, C), bf)
    for a in range(3):
        for m in range(4):
            row = (a * 4 + m) * C
            for par in range(2):
                b = m - par
                if 0 <= b <= 2:
                    if adjoint:
                        block = k_ref[(2 - a) * 3 + (2 - b)].T
                    else:
                        block = k_ref[a * 3 + b]
                else:
                    block = zero
                t_ref[row : row + C, par * C : (par + 1) * C] = block


def put_padded(p_ref, j, v, y0, count):
    vb = v.astype(bf).reshape(count, NS, C)
    spots = [(j + 1, vb)]
    if j == NJ - 1:
        spots.append((0, pltpu.roll(v.reshape(count, NS, C), 1, 1).astype(bf)))
    if j == 0:
        spots.append((NJ + 1, pltpu.roll(v.reshape(count, NS, C), NS - 1, 1).astype(bf)))
    for slot, value in spots:
        p_ref[slot, pl.ds(y0 + 1, count)] = value
    return vb


def wrap_rows(p_ref):
    for slot in range(NJ + 2):
        p_ref[slot, 0] = p_ref[slot, H]
        p_ref[slot, H + 1] = p_ref[slot, 1]


def piece(p_ref, slot, a, y0, count):
    return p_ref[slot, pl.ds(a + y0, count)].reshape(count * NS, C)


def conv_rows(p_ref, t_ref, q, y0, count):
    left = jnp.concatenate(
        [piece(p_ref, 2 * q + m, a, y0, count) for a in range(3) for m in range(4)], axis=1
    )
    return jnp.dot(left, t_ref[...], preferred_element_type=f32)


def run(main, *others):
    main = list(main)
    rest = [step for other in others for step in other]
    done = 0
    for i, step in enumerate(main):
        step()
        upto = (i + 1) * len(rest) // len(main)
        for other in rest[done:upto]:
            other()
        done = upto


def weight_grad(xt_ref, at, p_ref, acc_ref, which):
    def step(a, n):
        total = None
        for q in range(2):
            right = jnp.concatenate(
                [piece(p_ref, 2 * q + 2 * n + m, a, 0, H) for m in range(2)], axis=1
            )
            part = jnp.dot(xt_ref[at, q], right, preferred_element_type=f32)
            total = part if total is None else total + part
        acc_ref[which, a, :, n * 2 * C : (n + 1) * 2 * C] += total

    return [functools.partial(step, a, n) for a in range(3) for n in range(2)]


def emit_weight_grad(acc_ref, which, out_ref):
    for a in range(3):
        for b in range(3):
            total = None
            for par in range(2):
                m = par + 2 - b
                block = acc_ref[which, 2 - a, par * C : (par + 1) * C, m * C : (m + 1) * C]
                total = block if total is None else total + block
            out_ref[which, (a * 3 + b) * C : (a * 3 + b + 1) * C, :] = total


def finish_stats(s1, s2, shift, alpha, bias, extra):
    inv = 1.0 / PIX
    s1 = jnp.sum(s1, axis=0, keepdims=True) * inv
    s2 = jnp.sum(s2, axis=0, keepdims=True) * inv
    mean = shift + s1
    var = jnp.maximum(s2 - s1 * s1, 0.0)
    mean_v = alpha * (mean + bias) + extra
    mu = group_sum(mean_v) * (1.0 / 16)
    centred = mean_v - mu
    group_var = group_sum(alpha * alpha * var + centred * centred) * (1.0 / 16)
    rstd = lax.rsqrt(group_var + norm_epsilon)
    return mean, var, mean_v, mu, rstd


def pick(index, options):
    chosen = options[0]
    for k in range(1, len(options)):
        chosen = jnp.where(index == k, options[k], chosen)
    return chosen


def chunks(count):
    return [(j, y0) for j in range(NJ) for y0 in range(0, H, count)]


def forward_kernel(
    groups,
    me_ref,
    *refs,
):
    f_refs, refs = refs[:groups], refs[groups:]
    forward_items(groups, me_ref[0], f_refs, *refs)


def forward_items(
    groups,
    me,
    f_refs,
    perm_ref,
    tin_ref,
    k_ref,
    vec_ref,
    item_ref,
    lifted_ref,
    conv_ref,
    x1t_ref,
    x2t_ref,
    im_ref,
    stat_ref,
    *rest,
):
    out_refs, scratch = rest[:groups], rest[groups:]
    t1_ref, t2_ref = scratch[:2]
    pads = (scratch[2:4], scratch[4:6])
    z_refs = scratch[6:8]
    own = C // groups

    @pl.when(pl.program_id(0) == 0)
    def _():
        band_weights(k_ref.at[0], t1_ref, False)
        band_weights(k_ref.at[1], t2_ref, False)

    def vec(i):
        return vec_ref[i : i + 1, :]

    def item(n):
        state = {}
        p1_ref, p2_ref = pads[n]
        z_ref = z_refs[n]

        def lift():
            parts = [ref[n].astype(f32) for ref in f_refs]
            raw = jnp.concatenate(
                [
                    pick(me, [parts[(g - k) % groups] for g in range(groups)])
                    for k in range(groups)
                ],
                axis=1,
            )
            rows = jnp.concatenate([raw[:, i * 512 : (i + 1) * 512] for i in range(8)], axis=0)
            spread = jnp.dot(rows.astype(bf), perm_ref[...], preferred_element_type=f32)
            lane = lax.broadcasted_iota(jnp.int32, (64, 128), 1) % NS
            cols = [spread[:, j * 128 : (j + 1) * 128] for j in range(NJ)]
            before = jnp.where(
                lane == 0, pltpu.roll(cols[3], 128 - 15, 1), pltpu.roll(cols[3], 1, 1)
            )
            after = jnp.where(
                lane == NS - 1, pltpu.roll(cols[0], 15, 1), pltpu.roll(cols[0], 127, 1)
            )
            taps = []
            for v in [before] + cols + [after]:
                taps.append(jnp.concatenate([v[i * 8 : (i + 1) * 8, :] for i in range(8)], axis=1))
            stack = jnp.concatenate(taps, axis=0)
            up = pltpu.roll(stack, NS, 1)
            down = pltpu.roll(stack, ROWS - NS, 1)
            im_ref[n] = jnp.concatenate([up, stack, down], axis=0).astype(bf)

        def clear():
            state["s1"] = jnp.zeros((8, C), f32)
            state["s2"] = jnp.zeros((8, C), f32)
            state["shift"] = None

        def gather_stats(x):
            if state["shift"] is None:
                state["shift"] = x[0:1, :]
            x = x - state["shift"]
            state["s1"] = state["s1"] + rows8(x)
            state["s2"] = state["s2"] + rows8(x * x)

        def conv_in(part):
            if part == 0:
                clear()
            left = im_ref[n, :, part * 256 : (part + 1) * 256]
            r = lax.dot_general(
                left, tin_ref[...], (((0,), (0,)), ((), ())), preferred_element_type=f32
            )
            for j in range(NJ):
                x = r[:, j * C : (j + 1) * C]
                lifted_ref[n, j, part * 256 : (part + 1) * 256, :] = x.astype(bf)
                gather_stats(x)

        def first_stats():
            one = jnp.ones((1, C), f32)
            zero = jnp.zeros((1, C), f32)
            mean, var, mean_v, mu, rstd = finish_stats(
                state["s1"], state["s2"], state["shift"], one, vec(0), zero
            )
            state["scale"] = rstd * vec(1)
            state["base"] = (mean_v - mu - mean) * state["scale"] + vec(2)
            state["one"] = [mean, var, mu, rstd]

        def normal(src_ref, p_ref, xt_ref, count, j, y0):
            at = slice(y0 * NS, (y0 + count) * NS)
            x = src_ref[n, j, at, :].astype(f32)
            v = gelu(x * state["scale"] + state["base"])
            vb = put_padded(p_ref, j, v, y0, count)
            xt_ref[n, j // 2, (j % 2) * C : (j % 2 + 1) * C, at] = vb.reshape(count * NS, C).T

        def conv_one(q, y0, count):
            if q == 0 and y0 == 0:
                clear()
            r = conv_rows(p1_ref, t1_ref, q, y0, count)
            for par in range(2):
                x = r[:, par * C : (par + 1) * C]
                conv_ref[n, 2 * q + par, y0 * NS : (y0 + count) * NS, :] = x.astype(bf)
                gather_stats(x)

        def second_stats():
            alpha = item_ref[n, 0:1, :]
            extra = item_ref[n, 1:2, :]
            mean, var, mean_v, mu, rstd = finish_stats(
                state["s1"], state["s2"], state["shift"], alpha, vec(3), extra
            )
            state["scale"] = rstd * alpha * vec(6)
            state["base"] = (mean_v - mu) * rstd * vec(6) - mean * state["scale"] + vec(7)
            stat_ref[n] = jnp.concatenate(state["one"] + [mean, var, mu, rstd], axis=0)

        def conv_two(q, y0, count):
            r = conv_rows(p2_ref, t2_ref, q, y0, count)
            add = vec(0) + vec(8)
            for par in range(2):
                j = 2 * q + par
                at = slice(y0 * NS, (y0 + count) * NS)
                x = r[:, par * C : (par + 1) * C] + lifted_ref[n, j, at, :].astype(f32) + add
                z_ref[pl.ds(y0 * W + j, count * NS, stride=NJ), :] = x

        def flip(i):
            at = slice(i * 128, (i + 1) * 128)
            t = z_ref[at, :].T
            for s in range(groups):
                chans = [(g + s) % groups * own for g in range(groups)]
                piece = pick(me, [t[c : c + own, :] for c in chans])
                out_refs[s][n, :, at] = piece.astype(out_refs[s].dtype)

        part = functools.partial
        small, big = 8, 16
        bands = [(q, y0) for q in range(2) for y0 in range(0, H, big)]
        return {
            "lift": [lift] + [part(conv_in, k) for k in range(4)] + [first_stats],
            "one": [part(normal, lifted_ref, p1_ref, x1t_ref, small, *c) for c in chunks(small)]
            + [part(wrap_rows, p1_ref)],
            "conv1": [part(conv_one, *b, big) for b in bands] + [second_stats],
            "two": [part(normal, conv_ref, p2_ref, x2t_ref, small, *c) for c in chunks(small)]
            + [part(wrap_rows, p2_ref)],
            "conv2": [part(conv_two, *b, big) for b in bands],
            "flip": [part(flip, i) for i in range(PIX // 128)],
        }

    a, b = item(0), item(1)
    run(a["lift"])
    run(a["one"])
    run(a["conv1"], b["lift"], b["one"])
    run(b["conv1"], a["two"])
    run(a["conv2"], b["two"])
    run(b["conv2"], a["flip"])
    run(b["flip"])


def first_back_kernel(groups, items, chained, me_ref, *refs):
    step = pl.program_id(0)
    me = me_ref[0]
    start_refs, refs = refs[:groups], refs[groups:]
    next_refs, refs = refs[:groups], refs[groups:]
    conv_ref, x1t_ref, x2t_ref, stat_ref, item_ref, vec_ref, k_ref = refs[:7]
    refs = refs[7:]
    if chained:
        before_ref, refs = refs[2], refs[3:]
    pc_ref, pd_ref, dk_ref, dvec_ref, ditem_ref, t2_ref, z_ref, d_ref, acc_ref = refs
    pc_ref, pd_ref = pc_ref.at[0], pd_ref.at[0]
    part = functools.partial
    small, big = 8, 16

    def flip(src_refs, i):
        at = slice(i * 128, (i + 1) * 128)
        parts = [ref[0, :, at] for ref in src_refs]
        t = jnp.concatenate(
            [pick(me, [parts[(g - k) % groups] for g in range(groups)]) for k in range(groups)],
            axis=0,
        )
        z_ref[at, :] = t.astype(f32).T

    @pl.when(step == 0)
    def _():
        band_weights(k_ref.at[1], t2_ref, True)
        acc_ref[...] = jnp.zeros_like(acc_ref)
        dvec_ref[...] = jnp.zeros_like(dvec_ref)
        run([part(flip, start_refs, i) for i in range(PIX // 128)])

    def vec(i):
        return vec_ref[i : i + 1, :]

    def stat(i):
        return stat_ref[0, i : i + 1, :]

    cot_sum = jnp.zeros((8, C), f32)
    for j, y0 in chunks(big):
        v = z_ref[pl.ds(y0 * W + j, big * NS, stride=NJ), :]
        cot_sum = cot_sum + rows8(v)
        put_padded(pc_ref, j, v, y0, big)
    cot_sum = jnp.sum(cot_sum, axis=0, keepdims=True)
    wrap_rows(pc_ref)

    alpha = item_ref[0, 0:1, :]
    extra = item_ref[0, 1:2, :]
    mean, var, mu, rstd = stat(4), stat(5), stat(6), stat(7)
    mean_v = alpha * (mean + vec(3)) + extra
    sb, sx, sg, mean_en, c1, c2, c3, total = norm_back(
        pc_ref, t2_ref, conv_ref, d_ref, mean, mean_v, mu, rstd, alpha, vec(6), vec(7)
    )
    d_scaling = (
        rstd * (vec(6) * sx - mean_en * (rstd * alpha * PIX) * var) + (mean + vec(3)) * total
    )
    ditem_ref[0] = jnp.concatenate([d_scaling, total, jnp.zeros((6, C), f32)], axis=0)
    zero = jnp.zeros((1, C), f32)
    dvec_ref[...] += jnp.concatenate(
        [alpha * total, d_scaling, total, sg, sb, cot_sum, zero, zero], axis=0
    )

    def spread(j, y0):
        at = slice(y0 * NS, (y0 + small) * NS)
        x = conv_ref[0, j, at, :].astype(f32) - mean
        put_padded(pd_ref, j, d_ref[j, at, :] * c1 + (x * c3 + c2), y0, small)

    run(
        weight_grad(x2t_ref, 0, pc_ref, acc_ref, 1),
        [part(spread, *c) for c in chunks(small)],
    )
    wrap_rows(pd_ref)
    run(
        weight_grad(x1t_ref, 0, pd_ref, acc_ref, 0),
        [part(flip, next_refs, i) for i in range(PIX // 128)],
    )

    @pl.when(step == items - 1)
    def _():
        emit_weight_grad(acc_ref, 0, dk_ref)
        emit_weight_grad(acc_ref, 1, dk_ref)
        if chained:
            dk_ref[...] += before_ref[...]


def norm_back(p_ref, t_ref, src_ref, d_ref, mean, mean_v, mu, rstd, alpha, gain, beta):
    big = 16
    slope = rstd * alpha
    centre = (mean_v - mu) * rstd
    scale = slope * gain
    base = centre * gain + beta
    sums = [jnp.zeros((8, C), f32), jnp.zeros((8, C), f32)]

    def conv(q, y0):
        r = conv_rows(p_ref, t_ref, q, y0, big)
        for par in range(2):
            j = 2 * q + par
            at = slice(y0 * NS, (y0 + big) * NS)
            x = src_ref[0, j, at, :].astype(f32) - mean
            d = r[:, par * C : (par + 1) * C] * gelu_slope(x * scale + base)
            d_ref[j, at, :] = d
            sums[0] = sums[0] + rows8(d)
            sums[1] = sums[1] + rows8(d * x)

    run([functools.partial(conv, q, y0) for q in range(2) for y0 in range(0, H, big)])
    sb = jnp.sum(sums[0], axis=0, keepdims=True)
    sx = jnp.sum(sums[1], axis=0, keepdims=True)
    sg = slope * sx + centre * sb
    inv = 1.0 / (16 * PIX)
    mean_e = group_sum(gain * sb) * inv
    mean_en = group_sum(gain * sg) * inv
    c1 = slope * gain
    c3 = -slope * slope * mean_en
    c2 = -slope * (mean_e + mean_en * centre)
    total = rstd * (gain * sb - PIX * mean_e - PIX * mean_en * centre)
    return sb, sx, sg, mean_en, c1, c2, c3, total


def second_back_kernel(
    groups,
    pc_ref,
    pd_ref,
    lifted_ref,
    im_ref,
    stat_ref,
    vec_ref,
    tin_ref,
    perm_ref,
    k_ref,
    field_ref,
    din_ref,
    dvec_ref,
    t1_ref,
    d_ref,
    low_ref,
):
    small = 8
    pc_ref, pd_ref = pc_ref.at[0], pd_ref.at[0]

    @pl.when(pl.program_id(0) == 0)
    def _():
        band_weights(k_ref.at[0], t1_ref, True)
        din_ref[...] = jnp.zeros_like(din_ref)
        dvec_ref[...] = jnp.zeros_like(dvec_ref)

    def vec(i):
        return vec_ref[i : i + 1, :]

    def stat(i):
        return stat_ref[0, i : i + 1, :]

    one = jnp.ones((1, C), f32)
    mean, mu, rstd = stat(0), stat(2), stat(3)
    sb, sx, sg, mean_en, c1, c2, c3, total = norm_back(
        pd_ref, t1_ref, lifted_ref, d_ref, mean, mean + vec(0), mu, rstd, one, vec(1), vec(2)
    )
    for j, y0 in chunks(small):
        at = slice(y0 * NS, (y0 + small) * NS)
        x = lifted_ref[0, j, at, :].astype(f32) - mean
        g = pc_ref[j + 1, y0 + 1 : y0 + 1 + small].reshape(small * NS, C).astype(f32)
        low_ref[at, j * C : (j + 1) * C] = (g + (d_ref[j, at, :] * c1 + (x * c3 + c2))).astype(bf)
    dvec_ref[...] += jnp.concatenate([total, sg, sb, jnp.zeros((5, C), f32)], axis=0)

    din_ref[...] += jnp.dot(im_ref[0], low_ref[...], preferred_element_type=f32)
    back = lax.dot_general(
        tin_ref[...], low_ref[...], (((1,), (1,)), ((), ())), preferred_element_type=f32
    )
    stack = (
        pltpu.roll(back[0:48], ROWS - NS, 1) + back[48:96] + pltpu.roll(back[96:144], NS, 1)
    )
    lane = lax.broadcasted_iota(jnp.int32, (64, 128), 1) % NS

    def tall(jj):
        v = stack[jj * 8 : (jj + 1) * 8, :]
        return jnp.concatenate([v[:, i * 128 : (i + 1) * 128] for i in range(8)], axis=0)

    before, after = tall(0), tall(NJ + 1)
    before = jnp.where(lane == NS - 1, pltpu.roll(before, 15, 1), pltpu.roll(before, 127, 1))
    after = jnp.where(lane == 0, pltpu.roll(after, 128 - 15, 1), pltpu.roll(after, 1, 1))
    cols = [tall(j + 1) for j in range(NJ)]
    cols[3] = cols[3] + before
    cols[0] = cols[0] + after
    rows = jnp.concatenate(cols, axis=1).astype(bf)
    spread = lax.dot_general(
        rows, perm_ref[...], (((1,), (1,)), ((), ())), preferred_element_type=f32
    )
    natural = jnp.concatenate([spread[i * 8 : (i + 1) * 8, :] for i in range(8)], axis=1)
    cells = PIX // groups
    for g in range(groups):
        field_ref[g, 0] = natural[:, g * cells : (g + 1) * cells].astype(bf)


def whole(shape):
    return pl.BlockSpec(shape, lambda i, *_: (0,) * len(shape))


def by_item(shape, count=1, start=0):
    return pl.BlockSpec((count,) + shape, lambda i, *_: (i + start,) + (0,) * len(shape))


def swap(x, axis, hops):
    size = lax.axis_size(axis)
    return lax.ppermute(x, axis, [(i, (i + hops) % size) for i in range(size)])


def all_sum(x, axes):
    for axis in axes:
        size = lax.axis_size(axis)
        bit = 1
        while bit < size:
            x = x + lax.ppermute(x, axis, [(i, i ^ bit) for i in range(size)])
            bit *= 2
    return x


def local(
    fields,
    slot_mask,
    noise_step,
    cotangent,
    in_weight,
    in_moment,
    in_square,
    mid_weight,
    mid_moment,
    mid_square,
    time_weight,
    time_moment,
    time_square,
    vec_params,
    vec_moment,
    vec_square,
):
    both = ("wide", "grp")
    groups = lax.axis_size("grp")
    devices = groups * lax.axis_size("wide")
    held = fields.shape[0]
    items = held // groups
    slots = fields.shape[1]
    own = cotangent.shape[1]
    cells = fields.shape[2]
    me = lax.axis_index("grp")
    first_item = me * items
    pair = 2
    halves = 2
    some = items // halves

    mask_float = slot_mask.astype(f32)[:, :, None]
    masked_low = (fields * mask_float).astype(bf)

    def to_peer(x, hops, start, count):
        at = lax.rem(me + hops, groups) * items + start
        return swap(lax.dynamic_slice_in_dim(x, at, count, 0), "grp", hops)

    field_parts = [masked_low] + [to_peer(masked_low, s, 0, items) for s in range(1, groups)]
    share = mid_weight.shape[0]
    copies = jnp.broadcast_to(mid_weight.astype(bf)[None], (devices, share, C))
    gathered = lax.all_to_all(copies, both, split_axis=0, concat_axis=0, tiled=True)
    inner_taps = gathered.reshape(2, TAPS, C, C)
    cot_parts = [
        [to_peer(cotangent, s, h * some, some) for s in range(1, groups)] for h in range(halves)
    ]

    taps_in = in_weight.astype(bf).reshape(3, 3, slots, C)
    tin = jnp.stack(
        [jnp.pad(taps_in, ((0, 0), (j, NJ - 1 - j), (0, 0), (0, 0))) for j in range(NJ)], axis=3
    ).reshape(3 * (NJ + 2) * slots, NJ * C)
    spot = jnp.arange(8 * W)
    goal = (spot % NJ) * 128 + (spot // W) * NS + (spot % W) // NJ
    perm = (goal[:, None] == spot[None, :]).astype(bf)

    steps = lax.dynamic_slice_in_dim(noise_step, first_item, items, 0)
    features = fourier(steps, time_weight.shape[0])
    scaling = jnp.dot(features, time_weight[:, :C], precision=highest) + vec_params[4][None, :]
    offset = jnp.dot(features, time_weight[:, C:], precision=highest) + vec_params[5][None, :]
    item_vec = jnp.stack([1.0 + scaling, offset] + [jnp.zeros_like(offset)] * 6, axis=1)
    vecs = jnp.pad(vec_params, ((0, 7), (0, 0)))

    act = jax.ShapeDtypeStruct((items, NJ, ROWS, C), bf)
    flat = jax.ShapeDtypeStruct((items, 2, 2 * C, ROWS), bf)
    taps_rows = 3 * (NJ + 2) * slots
    pad_shape = (NJ + 2, H + 2, NS, C)
    pads = jax.ShapeDtypeStruct((items,) + pad_shape, bf)
    row = jax.ShapeDtypeStruct((items, 8, C), f32)
    band = pltpu.VMEM((12 * C, 2 * C), bf)
    tall = pltpu.VMEM((PIX, C), f32)
    params = pltpu.CompilerParams(vmem_limit_bytes=VMEM_LIMIT)
    my_group = me.astype(jnp.int32).reshape(1)

    def work(count, size, moved):
        gain = 2 * TAPS * C * C * PIX
        return pl.CostEstimate(
            flops=int(count * size * gain * 2),
            bytes_accessed=int(count * moved * 2 * C * PIX),
            transcendentals=0,
        )

    def mine(shape, count, index):
        return pl.BlockSpec(
            (count,) + shape, lambda i, g: (g[0] * (items // count) + index(i), 0, 0)
        )

    lifted, first_conv, x1t, x2t, im, stats, block_out, *sends = pl.pallas_call(
        functools.partial(forward_kernel, groups),
        grid_spec=pltpu.PrefetchScalarGridSpec(
            num_scalar_prefetch=1,
            grid=(items // pair,),
            in_specs=[mine((slots, cells), pair, lambda i: i)]
            + [by_item((slots, cells), pair)] * (groups - 1)
            + [
                whole((8 * W, 8 * W)),
                whole((taps_rows, NJ * C)),
                whole((2, TAPS, C, C)),
                whole((16, C)),
                by_item((8, C), pair),
            ],
            out_specs=[
                by_item((NJ, ROWS, C), pair),
                by_item((NJ, ROWS, C), pair),
                by_item((2, 2 * C, ROWS), pair),
                by_item((2, 2 * C, ROWS), pair),
                by_item((taps_rows, ROWS), pair),
                by_item((8, C), pair),
                mine((own, PIX), pair, lambda i: i),
            ]
            + [by_item((own, PIX), pair)] * (groups - 1),
            scratch_shapes=[band] * 2 + [pltpu.VMEM(pad_shape, bf)] * 4 + [tall] * 2,
        ),
        out_shape=[
            act,
            act,
            flat,
            flat,
            jax.ShapeDtypeStruct((items, taps_rows, ROWS), bf),
            row,
            jax.ShapeDtypeStruct((held, own, PIX), f32),
        ]
        + [jax.ShapeDtypeStruct((items, own, PIX), bf)] * (groups - 1),
        compiler_params=params,
        cost_estimate=work(items, 2.1, 7.5),
        name="forward_items",
    )(my_group, *field_parts, perm, tin, inner_taps, vecs, item_vec)

    for s in range(1, groups):
        source = lax.rem(me + groups - s, groups) * items
        arrived = swap(sends[s - 1], "grp", s)
        block_out = lax.dynamic_update_slice(block_out, arrived.astype(f32), (source, 0, 0))

    pc = pd = mid_grad = None
    mid_vecs = 0.0
    item_grads = []
    for h in range(halves):
        start = h * some
        chained = h > 0
        cot = [cotangent] + cot_parts[h]
        extra = [pc, pd, mid_grad] if chained else []
        any_spec = pl.BlockSpec(memory_space=pl.ANY)

        def after(i):
            return jnp.minimum(i + 1, some - 1)

        def cot_specs(index, start=start):
            return [mine((own, PIX), 1, lambda i: index(i) + start)] + [
                pl.BlockSpec((1, own, PIX), lambda i, g: (index(i), 0, 0))
            ] * (groups - 1)

        pc, pd, mid_grad, dvec, ditem = pl.pallas_call(
            functools.partial(first_back_kernel, groups, some, chained),
            grid_spec=pltpu.PrefetchScalarGridSpec(
                num_scalar_prefetch=1,
                grid=(some,),
                in_specs=cot_specs(lambda i: 0)
                + cot_specs(after)
                + [
                    by_item((NJ, ROWS, C), 1, start),
                    by_item((2, 2 * C, ROWS), 1, start),
                    by_item((2, 2 * C, ROWS), 1, start),
                    by_item((8, C), 1, start),
                    by_item((8, C), 1, start),
                    whole((16, C)),
                    whole((2, TAPS, C, C)),
                ]
                + ([any_spec, any_spec, whole((2, TAPS * C, C))] if chained else []),
                out_specs=[
                    by_item(pad_shape, 1, start),
                    by_item(pad_shape, 1, start),
                    whole((2, TAPS * C, C)),
                    whole((8, C)),
                    by_item((8, C), 1),
                ],
                scratch_shapes=[
                    band,
                    tall,
                    pltpu.VMEM((NJ, ROWS, C), f32),
                    pltpu.VMEM((2, 3, 2 * C, 4 * C), f32),
                ],
            ),
            out_shape=[
                pads,
                pads,
                jax.ShapeDtypeStruct((2, TAPS * C, C), f32),
                jax.ShapeDtypeStruct((8, C), f32),
                jax.ShapeDtypeStruct((some, 8, C), f32),
            ],
            input_output_aliases={2 * groups + 8: 0, 2 * groups + 9: 1} if chained else {},
            compiler_params=params,
            cost_estimate=work(some, 3.1, 7.2),
            name="first_back_items",
        )(my_group, *cot, *cot, first_conv, x1t, x2t, stats, item_vec, vecs, inner_taps, *extra)
        mid_vecs = mid_vecs + dvec
        item_grads.append(ditem)
    ditem = jnp.concatenate(item_grads, axis=0)

    field_low, din, outer_vecs = pl.pallas_call(
        functools.partial(second_back_kernel, groups),
        grid=(items,),
        out_shape=[
            jax.ShapeDtypeStruct((groups, items, slots, cells), bf),
            jax.ShapeDtypeStruct((taps_rows, NJ * C), f32),
            jax.ShapeDtypeStruct((8, C), f32),
        ],
        in_specs=[
            by_item(pad_shape),
            by_item(pad_shape),
            by_item((NJ, ROWS, C)),
            by_item((taps_rows, ROWS)),
            by_item((8, C)),
            whole((16, C)),
            whole((taps_rows, NJ * C)),
            whole((8 * W, 8 * W)),
            whole((2, TAPS, C, C)),
        ],
        out_specs=[
            pl.BlockSpec((groups, 1, slots, cells), lambda i: (0, i, 0, 0)),
            whole((taps_rows, NJ * C)),
            whole((8, C)),
        ],
        scratch_shapes=[
            band,
            pltpu.VMEM((NJ, ROWS, C), f32),
            pltpu.VMEM((ROWS, NJ * C), bf),
        ],
        compiler_params=params,
        cost_estimate=work(items, 1.2, 4.6),
        name="second_back_items",
    )(pc, pd, lifted, im, stats, vecs, tin, perm, inner_taps)

    field_half = lax.all_to_all(field_low, "grp", split_axis=0, concat_axis=0, tiled=True)
    field_grad = field_half.reshape(held, slots, cells).astype(f32) * mask_float

    din = din.reshape(3, NJ + 2, slots, NJ, C)
    grad_in = sum(din[:, j : j + 3, :, j, :] for j in range(NJ)).reshape(TAPS * slots, C)
    time_grad = lax.dot_general(
        features,
        jnp.concatenate([ditem[:, 0, :], ditem[:, 1, :]], axis=1),
        (((0,), (0,)), ((), ())),
        precision=highest,
    )
    small = jnp.concatenate([time_grad.reshape(-1, C), mid_vecs], axis=0)
    count = small.shape[0]
    each = -(-count // devices)
    small = jnp.pad(small, ((0, each * devices - count), (0, 0))).reshape(devices, each, C)
    parts = jnp.concatenate([mid_grad.reshape(devices, share, C), small], axis=1)
    parts = lax.all_to_all(parts, both, split_axis=0, concat_axis=0, tiled=True)
    summed = jnp.sum(parts, axis=0)
    mid_total = summed[:share]
    spread = jnp.broadcast_to(summed[share:][None], (devices, each, C))
    spread = lax.all_to_all(spread, both, split_axis=0, concat_axis=0, tiled=True)
    spread = spread.reshape(devices * each, C)
    time_total = spread[: 2 * C].reshape(time_weight.shape)
    mid_vecs = spread[2 * C : 2 * C + 8]
    last = all_sum(jnp.concatenate([grad_in, outer_vecs], axis=0), both)
    in_total = last[: TAPS * slots]
    outer_vecs = last[TAPS * slots :]
    cot_row = mid_vecs[5:6]
    vec_total = jnp.concatenate(
        [outer_vecs[0:1] + cot_row, outer_vecs[1:3], mid_vecs[0:5], cot_row], axis=0
    )

    step_float = jnp.float32(STEP)
    in_new, in_first, in_second = adam_update(
        in_weight, in_total, in_moment, in_square, rate_in, step_float
    )
    mid_new, mid_first, mid_second = adam_update(
        mid_weight, mid_total, mid_moment, mid_square, rate_mid, step_float
    )
    time_new, time_first, time_second = adam_update(
        time_weight, time_total, time_moment, time_square, rate_time, step_float
    )
    vec_new, vec_first, vec_second = adam_update(
        vec_params, vec_total, vec_moment, vec_square, rate_vecs, step_float
    )
    return (
        block_out,
        field_grad,
        in_new,
        in_first,
        in_second,
        in_new.astype(bf),
        mid_new,
        mid_first,
        mid_second,
        mid_new.astype(bf),
        time_new,
        time_first,
        time_second,
        vec_new,
        vec_first,
        vec_second,
    )


def solution(mesh):
    rows = P(("wide", "grp"), None)
    return jax.shard_map(
        local,
        mesh=mesh,
        in_specs=(
            P("wide", None, "grp"),
            P("wide", None),
            P("wide"),
            P("wide", "grp", None),
            P(),
            P(),
            P(),
            rows,
            rows,
            rows,
            P(),
            P(),
            P(),
            P(),
            P(),
            P(),
        ),
        out_specs=(
            P("wide", "grp", None),
            P("wide", None, "grp"),
            P(),
            P(),
            P(),
            P(),
            rows,
            rows,
            rows,
            rows,
            P(),
            P(),
            P(),
            P(),
            P(),
            P(),
        ),
        check_vma=False,
    )
```

time: 3020 us -> 254 us (0.08)
  local copies, waits for them, and re-layouts: 1100 us -> 9.86 us
  matrix products: 771 us -> 0.82 us
  other arithmetic: 579 us -> 21.5 us
  waiting for transfers between devices: 245 us -> 31.9 us
  blocking collectives: 209 us -> 0 us
  Pallas kernels: 0 us -> 161 us
  starting transfers between devices: 84.4 us -> 27.8 us
    dot_general x85 -> x3, matrix products: 771 us -> 0.82 us  [the longest x1 0.38 us: local(): lax.dot_general(features, jnp.concatenate([ditem[:, 0, :], ditem[:, 1, :]...]
    slice x24 -> x5, local copies, waits for them, and re-layouts: 305 us -> 0.03 us  [the longest x1 0.01 us: local(): time_total = spread[:2 * C].reshape(time_weight.shape)]
    concatenate x32 -> x3, other arithmetic: 289 us -> 3.16 us  [the longest x1 2.45 us: local(): jnp.concatenate([mid_grad.reshape(devices, share, C), small], axis=1)]
    unnamed x307 -> x33, local copies, waits for them, and re-layouts: 273 us -> 1.62 us
    convert_element_type x15 -> x1, local copies, waits for them, and re-layouts: 194 us -> 0.07 us  [local(): mask_float = slot_mask.astype(f32)[:, :, None]]
    all_to_all x10 -> x0, local copies, waits for them, and re-layouts: 166 us -> none  [the longest x7 131 us: to_rows(): lax.all_to_all(values, 'grp', split_axis=2, concat_axis=1, tiled=True)]
    pallas_call x0 -> x4, Pallas kernels: none -> 161 us  [the longest x2 69 us: local(): pl.pallas_call(functools.partial(first_back_kernel, groups, some, chained...]
    all_gather x1 -> x0, blocking collectives: 154 us -> none  [local(): lax.all_gather(mid_weight.astype(jnp.bfloat16), ('wide', 'grp'), axis=0,...]
  transfers between devices with their start and end apart: 23 -> 13, of which waited for: 5 -> 8; matrix products, arithmetic and copies ran while one was open for 48% -> 9% of each run, Pallas kernels for 0% -> 63%
where the time goes in v1:
time: 254 us
  Pallas kernels  161 us (63%)
  waiting for transfers between devices  31.9 us (13%)
  starting transfers between devices  27.8 us (11%)
  other arithmetic  21.5 us (8%)
  local copies, waits for them, and re-layouts  9.86 us (4%)
    pallas_call x2, Pallas kernels, local(): pl.pallas_call(functools.partial(first_back_kernel, groups, some, chained...  69 us
    pallas_call x1, Pallas kernels, local(): pl.pallas_call(functools.partial(forward_kernel, groups), grid_spec=pltpu...  49.7 us
    pallas_call x1, Pallas kernels, local(): pl.pallas_call(functools.partial(second_back_kernel, groups), grid=(items...  42 us
    all_to_all x1, waiting for transfers between devices, local(): lax.all_to_all(spread, both, split_axis=0, concat_axis=0, tiled=True)  8.91 us
    ppermute x5, waiting for transfers between devices, all_sum(): x = x + lax.ppermute(x, axis, [(i, i ^ bit) for i in range(size)])  8.91 us
    all_to_all x1, waiting for transfers between devices, local(): lax.all_to_all(field_low, 'grp', split_axis=0, concat_axis=0, tiled=True)  7.29 us
    ppermute x4, starting transfers between devices, swap(): return lax.ppermute(x, axis, [(i, (i + hops) % size) for i in range(size)])  6.7 us
    dynamic_update_slice x1, other arithmetic, local(): lax.dynamic_update_slice(block_out, arrived.astype(f32), (source, 0, 0))  6.67 us
  transfers between devices with their start and end apart: 13, of which 8 were waited for; matrix products, arithmetic and copies ran while one was open for 9% of the time, Pallas kernels for 63%

profile of v1, /device:TPU:0, one launch (start us, length us, event | category | flops | bytes accessed | tf_op | source)
XLA Modules:
  0.0 253.6 jit_solution(12239998958905027227)
XLA Ops:
  1.4 1.3 multiply_convert_fusion.refs_0_
  2.8 0.8 constant_dynamic-slice_fusion.2
  3.6 3.0 %collective-permute-start = (bf16[8,8,2048]{2,1,0:T(8,128)(2,1)}, bf16[8,8,2048]{2,1,0:T(8,128)(2,1)}, u32[]{:S(2)}, u32[]{:S(2)}) collective-permute-start(bf16[8,8,2048]{2,1,0:T(8,128)(2,1)} %constant_dynamic-slice_fusion.2), channel_id=1, source_target_pairs={{0,1},{1,0},{2,3},{3,2},{4,5},{5,4},{6,7},{7,6},{8,9},{9,8},{10,11... | collective-permute-start | bytes 786440 | tf_op jit(solution)/shard_map/ppermute | solution.py:563
  7.3 0.9 broadcast_in_dim.4
  8.2 4.9 %all-to-all-start = ((bf16[32,72,128]{2,1,0:T(8,128)(2,1)}), bf16[32,72,128]{2,1,0:T(8,128)(2,1)S(1)}, u32[]{:S(2)}, u32[]{:S(2)}) async-start(bf16[32,72,128]{2,1,0:T(8,128)(2,1)} %broadcast_in_dim.4), calls=%async_computation | async-start | bytes 1179648 | tf_op jit(solution)/shard_map/all_to_all | solution.py:618
  13.2 4.1 %constant_dynamic-slice_fusion = (bf16[4,64,4096]{2,1,0:T(8,128)(2,1)}, bf16[4,64,4096]{2,1,0:T(8,128)(2,1)S(1)}) fusion(bf16[16,64,4096]{2,1,0:T(8,128)(2,1)} %refs_2_.3, s32[]{:T(128)S(6)} %select_n.54, s32[]{:T(128)S(6)} %select_n.60), kind=kLoop, calls=%fused_computation.77 | loop fusion | bytes 8388616 | tf_op jit(solution)/shard_map/dynamic_slice | solution.py:613
  17.3 1.8 collective-permute-start.3
  22.2 1.0 fusion.1.refs_2_.perm_ref
  23.2 6.3 %all-to-all-done = bf16[32,72,128]{2,1,0:T(8,128)(2,1)S(1)} async-done(((bf16[32,72,128]{2,1,0:T(8,128)(2,1)}), bf16[32,72,128]{2,1,0:T(8,128)(2,1)S(1)}, u32[]{:S(2)}, u32[]{:S(2)}) %all-to-all-start) | async-done | bytes 589856 | tf_op jit(solution)/shard_map/all_to_all | solution.py:618
  29.5 0.8 copy-done.1
  30.3 49.7 %forward_items.1 = (bf16[8,4,1024,128]{3,2,1,0:T(8,128)(2,1)}, bf16[8,4,1024,128]{3,2,1,0:T(8,128)(2,1)}, bf16[8,2,256,1024]{3,2,1,0:T(8,128)(2,1)}, bf16[8,2,25...) custom-call(s32[1]{0:T(128)} %bitcast.me_ref, ...), custom_call_target="tpu_custom_call" | custom-call | flops 40587440128 | bytes 62914560 | tf_op jit(solution)/shard_map/forward_items/pallas_call | solution.py:663
  80.1 1.7 collective-permute-start.1
  81.8 34.2 %first_back_items.2 = (bf16[8,6,66,16,128]{4,3,2,1,0:T(8,128)(2,1)}, bf16[8,6,66,16,128]{4,3,2,1,0:T(8,128)(2,1)}, f32[2,1152,128]{2,1,0:T(8,128)}, f32[8,128]{1,0:T(8,128)}, f32[4,8,128]{2,1,0:T(8,128)}) custom-call(s32[1]{0:T(128)} %bitcast.me_ref, bf16[16,64,4096]{2,1,0:T(8,128)(2,1)} %refs_2_.3, ...), custom_call_target="tpu_custom_call" | custom-call | flops 29957396480 | bytes 30198988 | tf_op jit(solution)/shard_map/first_back_items/pallas_call | solution.py:727
  116.7 34.8 %first_back_items.3 = (bf16[8,6,66,16,128]{4,3,2,1,0:T(8,128)(2,1)}, bf16[8,6,66,16,128]{4,3,2,1,0:T(8,128)(2,1)}, f32[2,1152,128]{2,1,0:T(8,128)}, f32[8,128]{1,0:T(8,128)}, f32[4,8,128]{2,1,0:T(8,128)}) custom-call(s32[1]{0:T(128)} %bitcast.me_ref, bf16[16,64,4096]{2,1,0:T(8,128)(2,1)} %refs_2_.3, ...), custom_call_target="tpu_custom_call", output_to_operand_aliasing={{0}: (12, {}), {1}: (13, {})} | custom-call | flops 29957396480 | bytes 30198988 | tf_op jit(solution)/shard_map/first_back_items/pallas_call | solution.py:727
  153.4 2.5 pad_maximum_fusion
  155.8 2.9 %all-to-all-start.2 = ((f32[32,81,128]{2,1,0:T(8,128)}), f32[32,81,128]{2,1,0:T(8,128)S(1)}, u32[]{:S(2)}, u32[]{:S(2)}) async-start(f32[32,81,128]{2,1,0:T(8,128)} %pad_maximum_fusion), calls=%async_computation.2 | async-start | bytes 2883584 | tf_op jit(solution)/shard_map/all_to_all | solution.py:824
  158.8 42.0 %second_back_items.1 = (bf16[2,8,8,2048]{3,2,1,0:T(8,128)(2,1)}, f32[144,512]{1,0:T(8,128)}, f32[8,128]{1,0:T(8,128)}) custom-call(bf16[8,6,66,16,128]{4,3,2,1,0:T(8,128)(2,1)} %get-tuple-element.46.pc_ref, bf16[8,6,66,16,128]{4,3,2,1,0:T(8,128)(2,1)} %get-tuple-element.47.pd_ref, bf16[8,4,1024,128]{3,2,1,0:T(8,128)(2,1)} %get-tuple-element.48.lifted_ref, ...), custom_call_target="tpu_custom_call" | custom-call | flops 23192823808 | bytes 38587596 | tf_op jit(solution)/shard_map/second_back_items/pallas_call | solution.py:774
  200.9 0.9 slice_add_fusion
  202.5 1.2 collective-permute-done.4
  204.4 1.4 collective-permute-start.5
  205.7 2.6 %collective-permute-done.5 = f32[80,128]{1,0:T(8,128)S(1)} collective-permute-done((f32[80,128]{1,0:T(8,128)S(1)}, f32[80,128]{1,0:T(8,128)S(1)}, u32[]{:S(2)}, u32[]{:S(2)}) %collective-permute-start.5) | collective-permute-done | bytes 40992 | tf_op jit(solution)/shard_map/ppermute | solution.py:571
  208.4 1.4 collective-permute-start.6
  209.8 2.6 %collective-permute-done.6 = f32[80,128]{1,0:T(8,128)S(1)} collective-permute-done((f32[80,128]{1,0:T(8,128)S(1)}, f32[80,128]{1,0:T(8,128)S(1)}, u32[]{:S(2)}, u32[]{:S(2)}) %collective-permute-start.6) | collective-permute-done | bytes 40992 | tf_op jit(solution)/shard_map/ppermute | solution.py:571
  212.4 2.4 collective-permute-start.7
  214.8 2.5 collective-permute-done.7
  217.3 1.4 collective-permute-start.8
  219.2 3.5 %all-to-all-start.1 = ((bf16[2,8,8,2048]{3,2,1,0:T(8,128)(2,1)}), bf16[2,8,8,2048]{3,2,1,0:T(8,128)(2,1)S(1)}, u32[]{:S(2)}, u32[]{:S(2)}) async-start(bf16[2,8,8,2048]{3,2,1,0:T(8,128)(2,1)} %get-tuple-element.50), calls=%async_computation.1 | async-start | bytes 1048576 | tf_op jit(solution)/shard_map/all_to_all | solution.py:808
  223.5 7.3 %all-to-all-done.1 = bf16[2,8,8,2048]{3,2,1,0:T(8,128)(2,1)S(1)} async-done(((bf16[2,8,8,2048]{3,2,1,0:T(8,128)(2,1)}), bf16[2,8,8,2048]{3,2,1,0:T(8,128)(2,1)S(1)}, u32[]{:S(2)}, u32[]{:S(2)}) %all-to-all-start.1) | async-done | bytes 524320 | tf_op jit(solution)/shard_map/all_to_all | solution.py:808
  231.5 3.2 %all-to-all-start.3 = ((f32[32,9,128]{2,1,0:T(8,128)}), f32[32,9,128]{2,1,0:T(8,128)S(1)}, u32[]{:S(2)}, u32[]{:S(2)}) async-start(f32[32,9,128]{2,1,0:T(8,128)} %broadcast_in_dim.5), calls=%async_computation.3 | async-start | bytes 524288 | tf_op jit(solution)/shard_map/all_to_all | solution.py:828
  234.7 1.1 convert_multiply_fusion
  236.4 8.9 %all-to-all-done.3 = f32[32,9,128]{2,1,0:T(8,128)S(1)} async-done(((f32[32,9,128]{2,1,0:T(8,128)}), f32[32,9,128]{2,1,0:T(8,128)S(1)}, u32[]{:S(2)}, u32[]{:S(2)}) %all-to-all-start.3) | async-done | bytes 147488 | tf_op jit(solution)/shard_map/all_to_all | solution.py:828
  246.9 6.7 %convert_dynamic-update-slice_fusion = f32[16,64,4096]{2,1,0:T(8,128)} fusion(f32[16,64,4096]{2,1,0:T(8,128)} %get-tuple-element.37, s32[]{:T(128)S(6)} %select_n.54, bf16[8,64,4096]{2,1,0:T(8,128)(2,1)} %collective-permute-done.1), kind=kLoop, calls=%fused_computation | loop fusion | flops 2097152 | bytes 12582916 | tf_op jit(solution)/shard_map/dynamic_update_slice | solution.py:707
  (85 shorter events, 12.8 us)
Async XLA Ops:
  2.8 14.5 %copy-start = (bf16[16,8,2048]{2,1,0:T(8,128)(2,1)}, bf16[16,8,2048]{2,1,0:T(8,128)(2,1)S(1)}, u32[]{:S(2)}) copy-start(bf16[16,8,2048]{2,1,0:T(8,128)(2,1)S(1)} %multiply_convert_fusion.refs_0_) | copy-start | bytes 1572868
  3.6 19.6 %collective-permute-start = (bf16[8,8,2048]{2,1,0:T(8,128)(2,1)}, bf16[8,8,2048]{2,1,0:T(8,128)(2,1)}, u32[]{:S(2)}, u32[]{:S(2)}) collective-permute-start(bf16[8,8,2048]{2,1,0:T(8,128)(2,1)} %constant_dynamic-slice_fusion.2), channel_id=1, source_target_pairs={{0,1},{1,0},{2,3},{3,2},{4,5},{5,4},{6,7},{7,6},{8,9},{9,8},{10,11... | collective-permute-start | bytes 786440 | tf_op jit(solution)/shard_map/ppermute | solution.py:563
  8.2 21.3 %all-to-all-start = ((bf16[32,72,128]{2,1,0:T(8,128)(2,1)}), bf16[32,72,128]{2,1,0:T(8,128)(2,1)S(1)}, u32[]{:S(2)}, u32[]{:S(2)}) async-start(bf16[32,72,128]{2,1,0:T(8,128)(2,1)} %broadcast_in_dim.4), calls=%async_computation | async-start | bytes 1179648 | tf_op jit(solution)/shard_map/all_to_all | solution.py:618
  13.1 6.2 %copy-start.7 = (f32[9,128]{1,0:T(8,128)S(1)}, f32[9,128]{1,0:T(8,128)}, u32[]{:S(2)}) copy-start(f32[9,128]{1,0:T(8,128)} %param.29) | copy-start | bytes 13828
  13.1 6.2 %copy-start.3 = (f32[72,128]{1,0:T(8,128)S(1)}, f32[72,128]{1,0:T(8,128)}, u32[]{:S(2)}) copy-start(f32[72,128]{1,0:T(8,128)} %param.20) | copy-start | bytes 110596
  13.1 6.2 %copy-start.15 = (s32[16]{0:T(128)S(1)}, s32[16]{0:T(128)}, u32[]{:S(2)}) copy-start(s32[16]{0:T(128)} %param.18) | copy-start | bytes 196
  13.2 7.3 %copy-start.2 = (f32[128,256]{1,0:T(8,128)S(1)}, f32[128,256]{1,0:T(8,128)}, u32[]{:S(2)}) copy-start(f32[128,256]{1,0:T(8,128)} %param.26) | copy-start | bytes 393220
  17.3 64.5 %collective-permute-start.3 = (bf16[4,64,4096]{2,1,0:T(8,128)(2,1)}, bf16[4,64,4096]{2,1,0:T(8,128)(2,1)}, u32[]{:S(2)}, u32[]{:S(2)}) collective-permute-start(bf16[4,64,4096]{2,1,0:T(8,128)(2,1)} %get-tuple-element.72), channel_id=1, source_target_pairs={{0,1},{1,0},{2,3},{3,2},{4,5},{5,4},{6,7},{7,6},{8,9},{9,8},{10,11... | collective-permute-start | bytes 6291464 | tf_op jit(solution)/shard_map/ppermute | solution.py:563
  19.1 97.7 %collective-permute-start.2 = (bf16[4,64,4096]{2,1,0:T(8,128)(2,1)S(1)}, bf16[4,64,4096]{2,1,0:T(8,128)(2,1)}, u32[]{:S(2)}, u32[]{:S(2)}) collective-permute-start(bf16[4,64,4096]{2,1,0:T(8,128)(2,1)S(1)} %get-tuple-element.73), channel_id=1, source_target_pairs={{0,1},{1,0},{2,3},{3,2},{4,5},{5,4},{6,7},{7,6},{8,9},{9,8},{10,11... | collective-permute-start | bytes 6291464 | tf_op jit(solution)/shard_map/ppermute | solution.py:563
  29.5 0.8 copy-start.1
  80.1 166.9 %collective-permute-start.1 = (bf16[8,64,4096]{2,1,0:T(8,128)(2,1)}, bf16[8,64,4096]{2,1,0:T(8,128)(2,1)}, u32[]{:S(2)}, u32[]{:S(2)}) collective-permute-start(bf16[8,64,4096]{2,1,0:T(8,128)(2,1)} %get-tuple-element.38), channel_id=1, source_target_pairs={{0,1},{1,0},{2,3},{3,2},{4,5},{5,4},{6,7},{7,6},{8,9},{9,8},{10,11... | collective-permute-start | bytes 12582920 | tf_op jit(solution)/shard_map/ppermute | solution.py:563
  116.7 35.9 %copy-start.14 = (f32[8,128]{1,0:T(8,128)S(1)}, f32[8,128]{1,0:T(8,128)}, u32[]{:S(2)}) copy-start(f32[8,128]{1,0:T(8,128)} %get-tuple-element.56) | copy-start | bytes 12292
  155.8 63.3 %all-to-all-start.2 = ((f32[32,81,128]{2,1,0:T(8,128)}), f32[32,81,128]{2,1,0:T(8,128)S(1)}, u32[]{:S(2)}, u32[]{:S(2)}) async-start(f32[32,81,128]{2,1,0:T(8,128)} %pad_maximum_fusion), calls=%async_computation.2 | async-start | bytes 2883584 | tf_op jit(solution)/shard_map/all_to_all | solution.py:824
  158.8 63.9 %copy-start.8 = (f32[72,128]{1,0:T(8,128)S(1)}, f32[72,128]{1,0:T(8,128)}, u32[]{:S(2)}) copy-start(f32[72,128]{1,0:T(8,128)} %param.22) | copy-start | bytes 110596
  158.8 63.9 %copy-start.9 = (f32[72,128]{1,0:T(8,128)S(1)}, f32[72,128]{1,0:T(8,128)}, u32[]{:S(2)}) copy-start(f32[72,128]{1,0:T(8,128)} %param.21) | copy-start | bytes 110596
  200.8 35.0 %copy-start.4 = (f32[72,128]{1,0:T(8,128)S(1)}, f32[72,128]{1,0:T(8,128)}, u32[]{:S(2)}) copy-start(f32[72,128]{1,0:T(8,128)} %param.23) | copy-start | bytes 110596
  200.8 35.0 %copy-start.10 = (f32[72,128]{1,0:T(8,128)S(1)}, f32[72,128]{1,0:T(8,128)}, u32[]{:S(2)}) copy-start(f32[72,128]{1,0:T(8,128)} %param.25) | copy-start | bytes 110596
  200.8 35.0 %copy-start.11 = (f32[72,128]{1,0:T(8,128)S(1)}, f32[72,128]{1,0:T(8,128)}, u32[]{:S(2)}) copy-start(f32[72,128]{1,0:T(8,128)} %param.24) | copy-start | bytes 110596
  200.8 44.7 %copy-start.12 = (f32[9,128]{1,0:T(8,128)S(1)}, f32[9,128]{1,0:T(8,128)}, u32[]{:S(2)}) copy-start(f32[9,128]{1,0:T(8,128)} %param.31) | copy-start | bytes 13828
  200.8 44.7 %copy-start.13 = (f32[9,128]{1,0:T(8,128)S(1)}, f32[9,128]{1,0:T(8,128)}, u32[]{:S(2)}) copy-start(f32[9,128]{1,0:T(8,128)} %param.30) | copy-start | bytes 13828
  200.8 45.3 %copy-start.5 = (f32[128,256]{1,0:T(8,128)S(1)}, f32[128,256]{1,0:T(8,128)}, u32[]{:S(2)}) copy-start(f32[128,256]{1,0:T(8,128)} %param.28) | copy-start | bytes 393220
  200.8 45.3 %copy-start.6 = (f32[128,256]{1,0:T(8,128)S(1)}, f32[128,256]{1,0:T(8,128)}, u32[]{:S(2)}) copy-start(f32[128,256]{1,0:T(8,128)} %param.27) | copy-start | bytes 393220
  202.5 1.2 collective-permute-start.4
  204.4 4.0 %collective-permute-start.5 = (f32[80,128]{1,0:T(8,128)S(1)}, f32[80,128]{1,0:T(8,128)S(1)}, u32[]{:S(2)}, u32[]{:S(2)}) collective-permute-start(f32[80,128]{1,0:T(8,128)S(1)} %fusion.31), channel_id=1, source_target_pairs={{0,4},{2,6},{4,0},{6,2},{8,12},{10,14},{12,8},{14,10},{16,20},{18,... | collective-permute-start | bytes 122888 | tf_op jit(solution)/shard_map/ppermute | solution.py:571
  208.4 4.0 %collective-permute-start.6 = (f32[80,128]{1,0:T(8,128)S(1)}, f32[80,128]{1,0:T(8,128)S(1)}, u32[]{:S(2)}, u32[]{:S(2)}) collective-permute-start(f32[80,128]{1,0:T(8,128)S(1)} %add.227), channel_id=1, source_target_pairs={{0,8},{2,10},{4,12},{6,14},{8,0},{10,2},{12,4},{14,6},{16,24},{18,... | collective-permute-start | bytes 122888 | tf_op jit(solution)/shard_map/ppermute | solution.py:571
  212.4 4.9 %collective-permute-start.7 = (f32[80,128]{1,0:T(8,128)S(1)}, f32[80,128]{1,0:T(8,128)S(1)}, u32[]{:S(2)}, u32[]{:S(2)}) collective-permute-start(f32[80,128]{1,0:T(8,128)S(1)} %add.228), channel_id=1, source_target_pairs={{0,16},{2,18},{4,20},{6,22},{8,24},{10,26},{12,28},{14,30},{16,0},... | collective-permute-start | bytes 122888 | tf_op jit(solution)/shard_map/ppermute | solution.py:571
  217.3 5.4 %collective-permute-start.8 = (f32[80,128]{1,0:T(8,128)S(1)}, f32[80,128]{1,0:T(8,128)S(1)}, u32[]{:S(2)}, u32[]{:S(2)}) collective-permute-start(f32[80,128]{1,0:T(8,128)S(1)} %add.229), channel_id=1, source_target_pairs={{0,1},{1,0},{2,3},{3,2},{4,5},{5,4},{6,7},{7,6},{8,9},{9,8},{10,11... | collective-permute-start | bytes 122888 | tf_op jit(solution)/shard_map/ppermute | solution.py:571
  219.2 11.6 %all-to-all-start.1 = ((bf16[2,8,8,2048]{3,2,1,0:T(8,128)(2,1)}), bf16[2,8,8,2048]{3,2,1,0:T(8,128)(2,1)S(1)}, u32[]{:S(2)}, u32[]{:S(2)}) async-start(bf16[2,8,8,2048]{3,2,1,0:T(8,128)(2,1)} %get-tuple-element.50), calls=%async_computation.1 | async-start | bytes 1048576 | tf_op jit(solution)/shard_map/all_to_all | solution.py:808
  231.5 13.9 %all-to-all-start.3 = ((f32[32,9,128]{2,1,0:T(8,128)}), f32[32,9,128]{2,1,0:T(8,128)S(1)}, u32[]{:S(2)}, u32[]{:S(2)}) async-start(f32[32,9,128]{2,1,0:T(8,128)} %broadcast_in_dim.5), calls=%async_computation.3 | async-start | bytes 524288 | tf_op jit(solution)/shard_map/all_to_all | solution.py:828

commit v2 on v1

--- a/solution.py
+++ b/solution.py
@@ -65,18 +65,16 @@
     return jnp.sum(v.reshape(v.shape[0] // 8, 8, v.shape[1]), axis=0)
 
 
-def gelu(x):
-    x2 = x * x
-    t = jnp.tanh(x * (GELU_C + (GELU_C * GELU_K) * x2))
-    h = 0.5 * x
-    return h + h * t
-
-
-def gelu_slope(x):
-    x2 = x * x
-    t = jnp.tanh(x * (GELU_C + (GELU_C * GELU_K) * x2))
-    q = (0.5 * GELU_C) + (1.5 * GELU_C * GELU_K) * x2
-    return (0.5 + 0.5 * t) + (x * q) * (1.0 - t * t)
+def gelu_of_half(w):
+    t = jnp.tanh(w * (2 * GELU_C + (8 * GELU_C * GELU_K) * (w * w)))
+    return w + w * t
+
+
+def slope_of_half(w):
+    w2 = w * w
+    t = jnp.tanh(w * (2 * GELU_C + (8 * GELU_C * GELU_K) * w2))
+    v = w * (2 * GELU_C + (24 * GELU_C * GELU_K) * w2)
+    return (1.0 + t) * (1.0 + (1.0 - t) * v)
 
 
 def band_weights(k_ref, t_ref, adjoint):
@@ -88,7 +86,7 @@
                 b = m - par
                 if 0 <= b <= 2:
                     if adjoint:
-                        block = k_ref[(2 - a) * 3 + (2 - b)].T
+                        block = k_ref[(2 - a) * 3 + (2 - b)].T * jnp.array(0.5, bf)
                     else:
                         block = k_ref[a * 3 + b]
                 else:
@@ -189,15 +187,17 @@
 
 def forward_kernel(
     groups,
+    early_steps,
     me_ref,
     *refs,
 ):
     f_refs, refs = refs[:groups], refs[groups:]
-    forward_items(groups, me_ref[0], f_refs, *refs)
+    forward_items(groups, early_steps, me_ref[0], f_refs, *refs)
 
 
 def forward_items(
     groups,
+    early_steps,
     me,
     f_refs,
     perm_ref,
@@ -213,7 +213,13 @@
     stat_ref,
     *rest,
 ):
-    out_refs, scratch = rest[:groups], rest[groups:]
+    own_ref, rest = rest[0], rest[1:]
+    early_refs, late_refs, scratch = (
+        rest[: groups - 1],
+        rest[groups - 1 : (groups - 1) * 2],
+        rest[(groups - 1) * 2 :],
+    )
+    is_early = pl.program_id(0) < early_steps
     t1_ref, t2_ref = scratch[:2]
     pads = (scratch[2:4], scratch[4:6])
     z_refs = scratch[6:8]
@@ -289,14 +295,15 @@
             mean, var, mean_v, mu, rstd = finish_stats(
                 state["s1"], state["s2"], state["shift"], one, vec(0), zero
             )
-            state["scale"] = rstd * vec(1)
-            state["base"] = (mean_v - mu - mean) * state["scale"] + vec(2)
+            scale = rstd * vec(1)
+            state["scale"] = 0.5 * scale
+            state["base"] = 0.5 * ((mean_v - mu - mean) * scale + vec(2))
             state["one"] = [mean, var, mu, rstd]
 
         def normal(src_ref, p_ref, xt_ref, count, j, y0):
             at = slice(y0 * NS, (y0 + count) * NS)
             x = src_ref[n, j, at, :].astype(f32)
-            v = gelu(x * state["scale"] + state["base"])
+            v = gelu_of_half(x * state["scale"] + state["base"])
             vb = put_padded(p_ref, j, v, y0, count)
             xt_ref[n, j // 2, (j % 2) * C : (j % 2 + 1) * C, at] = vb.reshape(count * NS, C).T
 
@@ -315,8 +322,9 @@
             mean, var, mean_v, mu, rstd = finish_stats(
                 state["s1"], state["s2"], state["shift"], alpha, vec(3), extra
             )
-            state["scale"] = rstd * alpha * vec(6)
-            state["base"] = (mean_v - mu) * rstd * vec(6) - mean * state["scale"] + vec(7)
+            scale = rstd * alpha * vec(6)
+            state["scale"] = 0.5 * scale
+            state["base"] = 0.5 * ((mean_v - mu) * rstd * vec(6) - mean * scale + vec(7))
             stat_ref[n] = jnp.concatenate(state["one"] + [mean, var, mu, rstd], axis=0)
 
         def conv_two(q, y0, count):
@@ -334,7 +342,13 @@
             for s in range(groups):
                 chans = [(g + s) % groups * own for g in range(groups)]
                 piece = pick(me, [t[c : c + own, :] for c in chans])
-                out_refs[s][n, :, at] = piece.astype(out_refs[s].dtype)
+                if s == 0:
+                    own_ref[n, :, at] = piece
+                    continue
+                piece = piece.astype(bf)
+                early_ref = early_refs[s - 1]
+                early_ref[n, :, at] = jnp.where(is_early, piece, early_ref[n, :, at])
+                late_refs[s - 1][n, :, at] = piece
 
         part = functools.partial
         small, big = 8, 16
@@ -422,7 +436,7 @@
 
     def spread(j, y0):
         at = slice(y0 * NS, (y0 + small) * NS)
-        x = conv_ref[0, j, at, :].astype(f32) - mean
+        x = conv_ref[0, j, at, :].astype(f32)
         put_padded(pd_ref, j, d_ref[j, at, :] * c1 + (x * c3 + c2), y0, small)
 
     run(
@@ -444,11 +458,12 @@
 
 
 def norm_back(p_ref, t_ref, src_ref, d_ref, mean, mean_v, mu, rstd, alpha, gain, beta):
-    big = 16
+    big = 8
     slope = rstd * alpha
     centre = (mean_v - mu) * rstd
     scale = slope * gain
-    base = centre * gain + beta
+    half_scale = 0.5 * scale
+    half_base = 0.5 * (centre * gain + beta - mean * scale)
     sums = [jnp.zeros((8, C), f32), jnp.zeros((8, C), f32)]
 
     def conv(q, y0):
@@ -456,22 +471,22 @@
         for par in range(2):
             j = 2 * q + par
             at = slice(y0 * NS, (y0 + big) * NS)
-            x = src_ref[0, j, at, :].astype(f32) - mean
-            d = r[:, par * C : (par + 1) * C] * gelu_slope(x * scale + base)
+            x = src_ref[0, j, at, :].astype(f32)
+            d = r[:, par * C : (par + 1) * C] * slope_of_half(x * half_scale + half_base)
             d_ref[j, at, :] = d
             sums[0] = sums[0] + rows8(d)
             sums[1] = sums[1] + rows8(d * x)
 
     run([functools.partial(conv, q, y0) for q in range(2) for y0 in range(0, H, big)])
     sb = jnp.sum(sums[0], axis=0, keepdims=True)
-    sx = jnp.sum(sums[1], axis=0, keepdims=True)
+    sx = jnp.sum(sums[1], axis=0, keepdims=True) - mean * sb
     sg = slope * sx + centre * sb
     inv = 1.0 / (16 * PIX)
     mean_e = group_sum(gain * sb) * inv
     mean_en = group_sum(gain * sg) * inv
     c1 = slope * gain
     c3 = -slope * slope * mean_en
-    c2 = -slope * (mean_e + mean_en * centre)
+    c2 = -slope * (mean_e + mean_en * centre) - c3 * mean
     total = rstd * (gain * sb - PIX * mean_e - PIX * mean_en * centre)
     return sb, sx, sg, mean_en, c1, c2, c3, total
 
@@ -516,7 +531,7 @@
     )
     for j, y0 in chunks(small):
         at = slice(y0 * NS, (y0 + small) * NS)
-        x = lifted_ref[0, j, at, :].astype(f32) - mean
+        x = lifted_ref[0, j, at, :].astype(f32)
         g = pc_ref[j + 1, y0 + 1 : y0 + 1 + small].reshape(small * NS, C).astype(f32)
         low_ref[at, j * C : (j + 1) * C] = (g + (d_ref[j, at, :] * c1 + (x * c3 + c2))).astype(bf)
     dvec_ref[...] += jnp.concatenate([total, sg, sb, jnp.zeros((5, C), f32)], axis=0)
@@ -563,13 +578,12 @@
     return lax.ppermute(x, axis, [(i, (i + hops) % size) for i in range(size)])
 
 
-def all_sum(x, axes):
-    for axis in axes:
-        size = lax.axis_size(axis)
-        bit = 1
-        while bit < size:
-            x = x + lax.ppermute(x, axis, [(i, i ^ bit) for i in range(size)])
-            bit *= 2
+def all_sum(x, axis, bit=1, end=None):
+    size = lax.axis_size(axis)
+    end = size if end is None else end
+    while bit < end:
+        x = x + lax.ppermute(x, axis, [(i, i ^ bit) for i in range(size)])
+        bit *= 2
     return x
 
 
@@ -608,9 +622,12 @@
     mask_float = slot_mask.astype(f32)[:, :, None]
     masked_low = (fields * mask_float).astype(bf)
 
-    def to_peer(x, hops, start, count):
+    def to_peer(x, hops, start, count, after=None):
         at = lax.rem(me + hops, groups) * items + start
-        return swap(lax.dynamic_slice_in_dim(x, at, count, 0), "grp", hops)
+        part = lax.dynamic_slice_in_dim(x, at, count, 0)
+        if after is not None:
+            part, _ = lax.optimization_barrier((part, after))
+        return swap(part, "grp", hops)
 
     field_parts = [masked_low] + [to_peer(masked_low, s, 0, items) for s in range(1, groups)]
     share = mid_weight.shape[0]
@@ -618,7 +635,11 @@
     gathered = lax.all_to_all(copies, both, split_axis=0, concat_axis=0, tiled=True)
     inner_taps = gathered.reshape(2, TAPS, C, C)
     cot_parts = [
-        [to_peer(cotangent, s, h * some, some) for s in range(1, groups)] for h in range(halves)
+        [
+            to_peer(cotangent, s, h * some, some, field_parts[-1] if h > 0 else None)
+            for s in range(1, groups)
+        ]
+        for h in range(halves)
     ]
 
     taps_in = in_weight.astype(bf).reshape(3, 3, slots, C)
@@ -660,8 +681,12 @@
             (count,) + shape, lambda i, g: (g[0] * (items // count) + index(i), 0, 0)
         )
 
+    steps = items // pair
+    early_steps = max(1, steps // 2)
+    late_steps = max(1, steps - early_steps)
+    early = early_steps * pair
     lifted, first_conv, x1t, x2t, im, stats, block_out, *sends = pl.pallas_call(
-        functools.partial(forward_kernel, groups),
+        functools.partial(forward_kernel, groups, early_steps),
         grid_spec=pltpu.PrefetchScalarGridSpec(
             num_scalar_prefetch=1,
             grid=(items // pair,),
@@ -683,7 +708,18 @@
                 by_item((8, C), pair),
                 mine((own, PIX), pair, lambda i: i),
             ]
-            + [by_item((own, PIX), pair)] * (groups - 1),
+            + [
+                pl.BlockSpec(
+                    (pair, own, PIX), lambda i, g: (jnp.minimum(i, early_steps - 1), 0, 0)
+                )
+            ]
+            * (groups - 1)
+            + [
+                pl.BlockSpec(
+                    (pair, own, PIX), lambda i, g: (jnp.maximum(i - early_steps, 0), 0, 0)
+                )
+            ]
+            * (groups - 1),
             scratch_shapes=[band] * 2 + [pltpu.VMEM(pad_shape, bf)] * 4 + [tall] * 2,
         ),
         out_shape=[
@@ -695,16 +731,16 @@
             row,
             jax.ShapeDtypeStruct((held, own, PIX), f32),
         ]
-        + [jax.ShapeDtypeStruct((items, own, PIX), bf)] * (groups - 1),
+        + [jax.ShapeDtypeStruct((early, own, PIX), bf)] * (groups - 1)
+        + [jax.ShapeDtypeStruct((late_steps * pair, own, PIX), bf)] * (groups - 1),
         compiler_params=params,
         cost_estimate=work(items, 2.1, 7.5),
         name="forward_items",
     )(my_group, *field_parts, perm, tin, inner_taps, vecs, item_vec)
 
-    for s in range(1, groups):
-        source = lax.rem(me + groups - s, groups) * items
-        arrived = swap(sends[s - 1], "grp", s)
-        block_out = lax.dynamic_update_slice(block_out, arrived.astype(f32), (source, 0, 0))
+    sent = [[swap(sends[s - 1], "grp", s) for s in range(1, groups)]]
+    late = sends[groups - 1 :] if early < items else []
+    sent.append([swap(x, "grp", s + 1) for s, x in enumerate(late)])
 
     pc = pd = mid_grad = None
     mid_vecs = 0.0
@@ -771,6 +807,14 @@
         item_grads.append(ditem)
     ditem = jnp.concatenate(item_grads, axis=0)
 
+    wide = lax.axis_size("wide")
+    small = jnp.concatenate([features, ditem[:, 0, :], ditem[:, 1, :], mid_vecs], axis=0)
+    small = jnp.broadcast_to(small[None], (wide,) + small.shape)
+    shares = groups * share
+    parts = jnp.concatenate([mid_grad.reshape(wide, shares, C), small], axis=1)
+    parts = lax.all_to_all(parts, "wide", split_axis=0, concat_axis=0, tiled=True)
+
+    stats, sent[0] = lax.optimization_barrier((stats, sent[0]))
     field_low, din, outer_vecs = pl.pallas_call(
         functools.partial(second_back_kernel, groups),
         grid=(items,),
@@ -805,31 +849,49 @@
         name="second_back_items",
     )(pc, pd, lifted, im, stats, vecs, tin, perm, inner_taps)
 
-    field_half = lax.all_to_all(field_low, "grp", split_axis=0, concat_axis=0, tiled=True)
-    field_grad = field_half.reshape(held, slots, cells).astype(f32) * mask_float
-
+    din, parts = lax.optimization_barrier((din, parts))
     din = din.reshape(3, NJ + 2, slots, NJ, C)
     grad_in = sum(din[:, j : j + 3, :, j, :] for j in range(NJ)).reshape(TAPS * slots, C)
-    time_grad = lax.dot_general(
-        features,
-        jnp.concatenate([ditem[:, 0, :], ditem[:, 1, :]], axis=1),
-        (((0,), (0,)), ((), ())),
-        precision=highest,
-    )
-    small = jnp.concatenate([time_grad.reshape(-1, C), mid_vecs], axis=0)
-    count = small.shape[0]
-    each = -(-count // devices)
-    small = jnp.pad(small, ((0, each * devices - count), (0, 0))).reshape(devices, each, C)
-    parts = jnp.concatenate([mid_grad.reshape(devices, share, C), small], axis=1)
-    parts = lax.all_to_all(parts, both, split_axis=0, concat_axis=0, tiled=True)
-    summed = jnp.sum(parts, axis=0)
-    mid_total = summed[:share]
-    spread = jnp.broadcast_to(summed[share:][None], (devices, each, C))
-    spread = lax.all_to_all(spread, both, split_axis=0, concat_axis=0, tiled=True)
-    spread = spread.reshape(devices * each, C)
-    time_total = spread[: 2 * C].reshape(time_weight.shape)
-    mid_vecs = spread[2 * C : 2 * C + 8]
-    last = all_sum(jnp.concatenate([grad_in, outer_vecs], axis=0), both)
+    small = parts[:, shares:]
+    all_features = small[:, :items].reshape(wide * items, C)
+    time_rows = [
+        lax.dot_general(
+            all_features,
+            small[:, k * items : (k + 1) * items].reshape(wide * items, C),
+            (((0,), (0,)), ((), ())),
+            precision=highest,
+        )
+        for k in (1, 2)
+    ]
+    rows_all = jnp.concatenate(time_rows + [jnp.sum(small[:, 3 * items :], axis=0)], axis=0)
+    partial = jnp.sum(parts[:, :shares], axis=0)
+    last = all_sum(jnp.concatenate([grad_in, outer_vecs], axis=0), "wide", 1, 2)
+    last, field_low, sent[0] = lax.optimization_barrier((last, field_low, sent[0]))
+    field_grad = jnp.zeros((held, slots, cells), f32)
+    for s in range(groups):
+        source = lax.rem(me + groups - s, groups) * items
+        block = lax.dynamic_index_in_dim(field_low, lax.rem(me + s, groups), 0, False)
+        if s > 0:
+            block = swap(block, "grp", s)
+        field_grad = lax.dynamic_update_slice(field_grad, block.astype(f32), (source, 0, 0))
+    field_grad = field_grad * mask_float
+
+    last = all_sum(last, "wide", 2)
+    rows_in = last.shape[0]
+    last, sent[1] = lax.optimization_barrier((last, sent[1]))
+    for start, arrived in ((0, sent[0]), (early, sent[1])):
+        for s, block in enumerate(arrived):
+            source = lax.rem(me + groups - s - 1, groups) * items
+            block_out = lax.dynamic_update_slice(
+                block_out, block.astype(f32), (source + start, 0, 0)
+            )
+    last = all_sum(jnp.concatenate([last, rows_all, partial], axis=0), "grp")
+    rows_all = last[rows_in : rows_in + rows_all.shape[0]]
+    time_total = jnp.concatenate([rows_all[:C], rows_all[C : 2 * C]], axis=1)
+    mid_vecs = rows_all[2 * C :]
+    partial = last[last.shape[0] - shares :].reshape(groups, share, C)
+    mid_total = lax.dynamic_index_in_dim(partial, me, 0, False)
+    last = last[:rows_in]
     in_total = last[: TAPS * slots]
     outer_vecs = last[TAPS * slots :]
     cot_row = mid_vecs[5:6]

time: 254 us -> 222 us (0.87)
  waiting for transfers between devices: 31.9 us -> 12.5 us
  Pallas kernels: 161 us -> 154 us
  starting transfers between devices: 27.8 us -> 24 us
    all_to_all x3 -> x1, waiting for transfers between devices: 16.7 us -> 0.01 us  [local(): lax.all_to_all(parts, 'wide', split_axis=0, concat_axis=0, tiled=True)]
    all_to_all x3 -> x1, starting transfers between devices: 9.6 us -> 4.01 us  [local(): lax.all_to_all(parts, 'wide', split_axis=0, concat_axis=0, tiled=True)]
    pallas_call x2, Pallas kernels: 69 us -> 65 us  [local(): pl.pallas_call(functools.partial(first_back_kernel, groups, some, chained...]
    ppermute x5, waiting for transfers between devices: 8.91 us -> 5.31 us  [all_sum(): x = x + lax.ppermute(x, axis, [(i, i ^ bit) for i in range(size)])]
    pallas_call x1, Pallas kernels: 42 us -> 38.6 us  [local(): pl.pallas_call(functools.partial(second_back_kernel, groups), grid=(items...]
    ppermute x4 -> x6, starting transfers between devices: 6.7 us -> 9.24 us  [swap(): return lax.ppermute(x, axis, [(i, (i + hops) % size) for i in range(size)])]
    dynamic_update_slice x1 -> x4, other arithmetic: 6.67 us -> 6.69 us  [the longest x2 6.6 us: local(): lax.dynamic_update_slice(block_out, block.astype(f32), (source + start, 0...]
  transfers between devices with their start and end apart: 13 -> 13, of which waited for: 8 -> 6; matrix products, arithmetic and copies ran while one was open for 9% -> 11% of each run, Pallas kernels for 63% -> 69%
where the time goes in v2:
time: 222 us; the launch traced here: 221 us
  Pallas kernels  154 us (69%)
  starting transfers between devices  24 us (11%)
  other arithmetic  19.5 us (9%)
  waiting for transfers between devices  12.5 us (6%)
  local copies, waits for them, and re-layouts  9.55 us (4%)
    pallas_call x2, Pallas kernels, local(): pl.pallas_call(functools.partial(first_back_kernel, groups, some, chained...  65 us
    pallas_call x1, Pallas kernels, local(): pl.pallas_call(functools.partial(forward_kernel, groups, early_steps), gr...  50.1 us
    pallas_call x1, Pallas kernels, local(): pl.pallas_call(functools.partial(second_back_kernel, groups), grid=(items...  38.6 us
    ppermute x6, starting transfers between devices, swap(): return lax.ppermute(x, axis, [(i, (i + hops) % size) for i in range(size)])  9.24 us
    dynamic_update_slice x2, other arithmetic, local(): lax.dynamic_update_slice(block_out, block.astype(f32), (source + start, 0...  6.6 us
    ppermute x5, starting transfers between devices, all_sum(): x = x + lax.ppermute(x, axis, [(i, i ^ bit) for i in range(size)])  5.9 us
    all_to_all x1, waiting for transfers between devices, local(): lax.all_to_all(copies, both, split_axis=0, concat_axis=0, tiled=True)  5.71 us
    ppermute x5, waiting for transfers between devices, all_sum(): x = x + lax.ppermute(x, axis, [(i, i ^ bit) for i in range(size)])  5.31 us
  transfers between devices with their start and end apart: 13, of which 6 were waited for; matrix products, arithmetic and copies ran while one was open for 11% of the time, Pallas kernels for 69%

profile of v2, /device:TPU:0, one launch (start us, length us, event | category | flops | bytes accessed | tf_op | source)
XLA Modules:
  0.0 221.5 jit_solution(7191547081391927415)
XLA Ops:
  1.4 1.3 multiply_convert_fusion.refs_0_
  2.8 3.0 %collective-permute-start = (bf16[8,8,2048]{2,1,0:T(8,128)(2,1)S(1)}, bf16[8,8,2048]{2,1,0:T(8,128)(2,1)S(1)}, u32[]{:S(2)}, u32[]{:S(2)}) collective-permute-start(bf16[8,8,2048]{2,1,0:T(8,128)(2,1)S(1)} %constant_dynamic-slice_fusion.2), channel_id=1, source_target_pairs={{0,1},{1,0},{2,3},{3,2},{4,5},{5,4},{6,7},{7,6},{8,9},{9,8},{10,11... | collective-permute-start | bytes 786440 | tf_op jit(solution)/shard_map/ppermute | solution.py:578
  5.9 0.9 broadcast_in_dim.6
  6.8 4.9 %all-to-all-start = ((bf16[32,72,128]{2,1,0:T(8,128)(2,1)}), bf16[32,72,128]{2,1,0:T(8,128)(2,1)S(1)}, u32[]{:S(2)}, u32[]{:S(2)}) async-start(bf16[32,72,128]{2,1,0:T(8,128)(2,1)} %broadcast_in_dim.6), calls=%async_computation | async-start | bytes 1179648 | tf_op jit(solution)/shard_map/all_to_all | solution.py:635
  11.7 4.8 %constant_dynamic-slice_fusion = (bf16[4,64,4096]{2,1,0:T(8,128)(2,1)}, bf16[4,64,4096]{2,1,0:T(8,128)(2,1)}) fusion(bf16[16,64,4096]{2,1,0:T(8,128)(2,1)} %refs_2_.3, s32[]{:T(128)S(6)} %select_n.70, s32[]{:T(128)S(6)} %select_n.76), kind=kLoop, calls=%fused_computation.77 | loop fusion | bytes 8388616 | tf_op jit(solution)/shard_map/dynamic_slice | solution.py:627
  16.5 1.8 collective-permute-start.2
  21.1 0.9 fusion.3.refs_2_.perm_ref
  22.4 5.7 %all-to-all-done = bf16[32,72,128]{2,1,0:T(8,128)(2,1)S(1)} async-done(((bf16[32,72,128]{2,1,0:T(8,128)(2,1)}), bf16[32,72,128]{2,1,0:T(8,128)(2,1)S(1)}, u32[]{:S(2)}, u32[]{:S(2)}) %all-to-all-start) | async-done | bytes 589856 | tf_op jit(solution)/shard_map/all_to_all | solution.py:635
  28.1 0.8 copy-done.1
  28.9 50.1 %forward_items.1 = (bf16[8,4,1024,128]{3,2,1,0:T(8,128)(2,1)}, bf16[8,4,1024,128]{3,2,1,0:T(8,128)(2,1)}, bf16[8,2,256,1024]{3,2,1,0:T(8,128)(2,1)}, bf16[8,2,25...) custom-call(s32[1]{0:T(128)} %bitcast.me_ref, ...), custom_call_target="tpu_custom_call" | custom-call | flops 40587440128 | bytes 62914560 | tf_op jit(solution)/shard_map/forward_items/pallas_call | solution.py:688
  79.0 1.7 collective-permute-start.3
  80.7 32.2 %first_back_items.2 = (bf16[8,6,66,16,128]{4,3,2,1,0:T(8,128)(2,1)}, bf16[8,6,66,16,128]{4,3,2,1,0:T(8,128)(2,1)}, f32[2,1152,128]{2,1,0:T(8,128)}, f32[8,128]{1,0:T(8,128)}, f32[4,8,128]{2,1,0:T(8,128)}) custom-call(s32[1]{0:T(128)} %bitcast.me_ref, bf16[16,64,4096]{2,1,0:T(8,128)(2,1)} %refs_2_.3, ...), custom_call_target="tpu_custom_call" | custom-call | flops 29957396480 | bytes 30198988 | tf_op jit(solution)/shard_map/first_back_items/pallas_call | solution.py:763
  113.0 0.7 constant_dynamic-update-slice_fusion.1
  113.7 32.8 %first_back_items.3 = (bf16[8,6,66,16,128]{4,3,2,1,0:T(8,128)(2,1)}, bf16[8,6,66,16,128]{4,3,2,1,0:T(8,128)(2,1)}, f32[2,1152,128]{2,1,0:T(8,128)}, f32[8,128]{1,0:T(8,128)}, f32[4,8,128]{2,1,0:T(8,128)}) custom-call(s32[1]{0:T(128)} %bitcast.me_ref, bf16[16,64,4096]{2,1,0:T(8,128)(2,1)} %refs_2_.3, ...), custom_call_target="tpu_custom_call", output_to_operand_aliasing={{0}: (12, {}), {1}: (13, {})} | custom-call | flops 29957396480 | bytes 30198988 | tf_op jit(solution)/shard_map/first_back_items/pallas_call | solution.py:763
  147.2 0.7 constant_dynamic-update-slice_fusion
  148.0 2.5 %pad_maximum_fusion = f32[16,176,128]{2,1,0:T(8,128)} fusion(f32[16,32,128]{2,1,0:T(8,128)S(1)} %broadcast_in_dim.7, f32[16,144,128]{2,1,0:T(8,128)} %bitcast.52), kind=kLoop, calls=%fused_computation.2 | loop fusion | flops 360448 | bytes 2883584 | tf_op jit(solution)/shard_map/concatenate | solution.py:814
  150.5 4.0 %all-to-all-start.1 = ((f32[16,176,128]{2,1,0:T(8,128)}), f32[16,176,128]{2,1,0:T(8,128)S(1)}, u32[]{:S(2)}, u32[]{:S(2)}) async-start(f32[16,176,128]{2,1,0:T(8,128)} %pad_maximum_fusion), calls=%async_computation.1 | async-start | bytes 2883584 | tf_op jit(solution)/shard_map/all_to_all | solution.py:815
  154.6 1.2 collective-permute-start.8
  155.8 1.5 collective-permute-done.3
  157.3 38.6 %second_back_items.1 = (bf16[2,8,8,2048]{3,2,1,0:T(8,128)(2,1)}, f32[144,512]{1,0:T(8,128)}, f32[8,128]{1,0:T(8,128)}) custom-call(bf16[8,6,66,16,128]{4,3,2,1,0:T(8,128)(2,1)} %get-tuple-element.57.pc_ref, bf16[8,6,66,16,128]{4,3,2,1,0:T(8,128)(2,1)} %get-tuple-element.58.pd_ref, bf16[8,4,1024,128]{3,2,1,0:T(8,128)(2,1)} %get-tuple-element.59.lifted_ref, ...), custom_call_target="tpu_custom_call" | custom-call | flops 23192823808 | bytes 38587596 | tf_op jit(solution)/shard_map/second_back_items/pallas_call | solution.py:818
  195.9 0.8 slice_add_fusion
  198.6 0.9 collective-permute-start.5
  199.5 1.3 collective-permute-start.9
  200.8 1.9 collective-permute-done.5
  202.7 1.9 collective-permute-start.6
  204.6 2.5 %convert_dynamic-update-slice_fusion.1 = f32[16,64,4096]{2,1,0:T(8,128)} fusion(f32[16,64,4096]{2,1,0:T(8,128)} %get-tuple-element.48, s32[]{:T(128)S(6)} %select_n.70, bf16[4,64,4096]{2,1,0:T(8,128)(2,1)S(1)} %collective-permute-done.3), kind=kLoop, calls=%fused_computation.1 | loop fusion | flops 1048576 | bytes 6291460 | tf_op jit(solution)/shard_map/dynamic_update_slice | solution.py:885
  207.1 2.2 collective-permute-start.7
  209.5 2.6 %collective-permute-done.7 = f32[80,128]{1,0:T(8,128)S(1)} collective-permute-done((f32[80,128]{1,0:T(8,128)S(1)}, f32[80,128]{1,0:T(8,128)S(1)}, u32[]{:S(2)}, u32[]{:S(2)}) %collective-permute-start.7) | collective-permute-done | bytes 40992 | tf_op jit(solution)/shard_map/ppermute | solution.py:585
  212.7 1.0 collective-permute-start.10
  213.7 4.1 %convert_dynamic-update-slice_fusion = f32[16,64,4096]{2,1,0:T(8,128)} fusion(f32[16,64,4096]{2,1,0:T(8,128)} %convert_dynamic-update-slice_fusion.1, s32[]{:T(128)S(6)} %select_n.76, bf16[4,64,4096]{2,1,0:T(8,128)(2,1)} %collective-permute-done.8), kind=kLoop, calls=%fused_computation | loop fusion | flops 1048576 | bytes 6291460 | tf_op jit(solution)/shard_map/dynamic_update_slice | solution.py:885
  217.9 1.1 broadcast_multiply_fusion
  219.3 0.8 multiply_subtract_fusion
  (103 shorter events, 9.0 us)
Async XLA Ops:
  0.6 5.2 %copy-start.7 = (f32[72,128]{1,0:T(8,128)S(1)}, f32[72,128]{1,0:T(8,128)}, u32[]{:S(2)}) copy-start(f32[72,128]{1,0:T(8,128)} %param.23) | copy-start | bytes 110596
  2.8 13.7 %copy-start = (bf16[16,8,2048]{2,1,0:T(8,128)(2,1)}, bf16[16,8,2048]{2,1,0:T(8,128)(2,1)S(1)}, u32[]{:S(2)}) copy-start(bf16[16,8,2048]{2,1,0:T(8,128)(2,1)S(1)} %multiply_convert_fusion.refs_0_) | copy-start | bytes 1572868
  2.8 19.3 %collective-permute-start = (bf16[8,8,2048]{2,1,0:T(8,128)(2,1)S(1)}, bf16[8,8,2048]{2,1,0:T(8,128)(2,1)S(1)}, u32[]{:S(2)}, u32[]{:S(2)}) collective-permute-start(bf16[8,8,2048]{2,1,0:T(8,128)(2,1)S(1)} %constant_dynamic-slice_fusion.2), channel_id=1, source_target_pairs={{0,1},{1,0},{2,3},{3,2},{4,5},{5,4},{6,7},{7,6},{8,9},{9,8},{10,11... | collective-permute-start | bytes 786440 | tf_op jit(solution)/shard_map/ppermute | solution.py:578
  6.8 21.3 %all-to-all-start = ((bf16[32,72,128]{2,1,0:T(8,128)(2,1)}), bf16[32,72,128]{2,1,0:T(8,128)(2,1)S(1)}, u32[]{:S(2)}, u32[]{:S(2)}) async-start(bf16[32,72,128]{2,1,0:T(8,128)(2,1)} %broadcast_in_dim.6), calls=%async_computation | async-start | bytes 1179648 | tf_op jit(solution)/shard_map/all_to_all | solution.py:635
  11.7 6.6 %copy-start.11 = (f32[9,128]{1,0:T(8,128)S(1)}, f32[9,128]{1,0:T(8,128)}, u32[]{:S(2)}) copy-start(f32[9,128]{1,0:T(8,128)} %param.29) | copy-start | bytes 13828
  11.7 6.6 %copy-start.5 = (f32[72,128]{1,0:T(8,128)S(1)}, f32[72,128]{1,0:T(8,128)}, u32[]{:S(2)}) copy-start(f32[72,128]{1,0:T(8,128)} %param.20) | copy-start | bytes 110596
  11.7 6.6 %copy-start.21 = (s32[16]{0:T(128)S(1)}, s32[16]{0:T(128)}, u32[]{:S(2)}) copy-start(s32[16]{0:T(128)} %param.18) | copy-start | bytes 196
  11.7 7.7 %copy-start.2 = (f32[128,256]{1,0:T(8,128)S(1)}, f32[128,256]{1,0:T(8,128)}, u32[]{:S(2)}) copy-start(f32[128,256]{1,0:T(8,128)} %param.26) | copy-start | bytes 393220
  16.5 64.2 %collective-permute-start.2 = (bf16[4,64,4096]{2,1,0:T(8,128)(2,1)}, bf16[4,64,4096]{2,1,0:T(8,128)(2,1)}, u32[]{:S(2)}, u32[]{:S(2)}) collective-permute-start(bf16[4,64,4096]{2,1,0:T(8,128)(2,1)} %get-tuple-element.94), channel_id=1, source_target_pairs={{0,1},{1,0},{2,3},{3,2},{4,5},{5,4},{6,7},{7,6},{8,9},{9,8},{10,11... | collective-permute-start | bytes 6291464 | tf_op jit(solution)/shard_map/ppermute | solution.py:578
  22.1 6.0 %copy-start.20 = (bf16[8,8,2048]{2,1,0:T(8,128)(2,1)}, bf16[8,8,2048]{2,1,0:T(8,128)(2,1)S(1)}, u32[]{:S(2)}) copy-start(bf16[8,8,2048]{2,1,0:T(8,128)(2,1)S(1)} %collective-permute-done.refs_1_) | copy-start | bytes 786436
  22.1 91.6 %collective-permute-start.1 = (bf16[4,64,4096]{2,1,0:T(8,128)(2,1)}, bf16[4,64,4096]{2,1,0:T(8,128)(2,1)}, u32[]{:S(2)}, u32[]{:S(2)}) collective-permute-start(bf16[4,64,4096]{2,1,0:T(8,128)(2,1)} %get-tuple-element.49), channel_id=1, source_target_pairs={{0,1},{1,0},{2,3},{3,2},{4,5},{5,4},{6,7},{7,6},{8,9},{9,8},{10,11... | collective-permute-start | bytes 6291464 | tf_op jit(solution)/shard_map/ppermute | solution.py:578
  79.0 78.3 %collective-permute-start.3 = (bf16[4,64,4096]{2,1,0:T(8,128)(2,1)}, bf16[4,64,4096]{2,1,0:T(8,128)(2,1)S(1)}, u32[]{:S(2)}, u32[]{:S(2)}) collective-permute-start(bf16[4,64,4096]{2,1,0:T(8,128)(2,1)} %get-tuple-element.61), channel_id=1, source_target_pairs={{0,1},{1,0},{2,3},{3,2},{4,5},{5,4},{6,7},{7,6},{8,9},{9,8},{10,11... | collective-permute-start | bytes 6291464 | tf_op jit(solution)/shard_map/ppermute | solution.py:578
  113.7 32.8 %copy-start.19 = (f32[8,128]{1,0:T(8,128)S(1)}, f32[8,128]{1,0:T(8,128)}, u32[]{:S(2)}) copy-start(f32[8,128]{1,0:T(8,128)} %get-tuple-element.67) | copy-start | bytes 12292
  150.5 45.3 %all-to-all-start.1 = ((f32[16,176,128]{2,1,0:T(8,128)}), f32[16,176,128]{2,1,0:T(8,128)S(1)}, u32[]{:S(2)}, u32[]{:S(2)}) async-start(f32[16,176,128]{2,1,0:T(8,128)} %pad_maximum_fusion), calls=%async_computation.1 | async-start | bytes 2883584 | tf_op jit(solution)/shard_map/all_to_all | solution.py:815
  154.6 57.5 %collective-permute-start.8 = (bf16[4,64,4096]{2,1,0:T(8,128)(2,1)}, bf16[4,64,4096]{2,1,0:T(8,128)(2,1)}, u32[]{:S(2)}, u32[]{:S(2)}) collective-permute-start(bf16[4,64,4096]{2,1,0:T(8,128)(2,1)} %get-tuple-element.75), channel_id=1, source_target_pairs={{0,1},{1,0},{2,3},{3,2},{4,5},{5,4},{6,7},{7,6},{8,9},{9,8},{10,11... | collective-permute-start | bytes 6291464 | tf_op jit(solution)/shard_map/ppermute | solution.py:578
  197.4 2.1 copy-start.4
  197.4 1.2 collective-permute-start.4
  198.6 4.1 %collective-permute-start.5 = (f32[80,128]{1,0:T(8,128)S(1)}, f32[80,128]{1,0:T(8,128)S(1)}, u32[]{:S(2)}, u32[]{:S(2)}) collective-permute-start(f32[80,128]{1,0:T(8,128)S(1)} %fusion.32), channel_id=1, source_target_pairs={{0,4},{2,6},{4,0},{6,2},{8,12},{10,14},{12,8},{14,10},{16,20},{18,... | collective-permute-start | bytes 122888 | tf_op jit(solution)/shard_map/ppermute | solution.py:585
  199.5 18.3 %collective-permute-start.9 = (bf16[8,8,2048]{2,1,0:T(8,128)(2,1)S(1)}, bf16[8,8,2048]{2,1,0:T(8,128)(2,1)S(1)}, u32[]{:S(2)}, u32[]{:S(2)}) collective-permute-start(bf16[8,8,2048]{2,1,0:T(8,128)(2,1)S(1)} %dynamic-slice_bitcast_fusion), channel_id=1, source_target_pairs={{0,1},{1,0},{2,3},{3,2},{4,5},{5,4},{6,7},{7,6},{8,9},{9,8},{10,11... | collective-permute-start | bytes 786440 | tf_op jit(solution)/shard_map/ppermute | solution.py:578
  202.7 4.4 %collective-permute-start.6 = (f32[80,128]{1,0:T(8,128)S(1)}, f32[80,128]{1,0:T(8,128)S(1)}, u32[]{:S(2)}, u32[]{:S(2)}) collective-permute-start(f32[80,128]{1,0:T(8,128)S(1)} %add.249), channel_id=1, source_target_pairs={{0,8},{2,10},{4,12},{6,14},{8,0},{10,2},{12,4},{14,6},{16,24},{18,... | collective-permute-start | bytes 122888 | tf_op jit(solution)/shard_map/ppermute | solution.py:585
  207.1 5.0 %collective-permute-start.7 = (f32[80,128]{1,0:T(8,128)S(1)}, f32[80,128]{1,0:T(8,128)S(1)}, u32[]{:S(2)}, u32[]{:S(2)}) collective-permute-start(f32[80,128]{1,0:T(8,128)S(1)} %add.250), channel_id=1, source_target_pairs={{0,16},{2,18},{4,20},{6,22},{8,24},{10,26},{12,28},{14,30},{16,0},... | collective-permute-start | bytes 122888 | tf_op jit(solution)/shard_map/ppermute | solution.py:585
  212.7 6.4 %collective-permute-start.10 = (f32[488,128]{1,0:T(8,128)S(1)}, f32[488,128]{1,0:T(8,128)S(1)}, u32[]{:S(2)}, u32[]{:S(2)}) collective-permute-start(f32[488,128]{1,0:T(8,128)S(1)} %constant_dynamic-update-slice_fusion.2), channel_id=1, source_target_pairs={{0,1},{1,0},{2,3},{3,2},{4,5},{5,4},{6,7},{7,6},{8,9},{9,8},{10,11... | collective-permute-start | bytes 749576 | tf_op jit(solution)/shard_map/ppermute | solution.py:585
  217.8 1.5 copy-start.9
  217.8 1.5 copy-start.10
  217.9 2.3 %copy-start.17 = (f32[9,128]{1,0:T(8,128)S(1)}, f32[9,128]{1,0:T(8,128)}, u32[]{:S(2)}) copy-start(f32[9,128]{1,0:T(8,128)} %param.31) | copy-start | bytes 13828
  217.9 2.2 %copy-start.18 = (f32[9,128]{1,0:T(8,128)S(1)}, f32[9,128]{1,0:T(8,128)}, u32[]{:S(2)}) copy-start(f32[9,128]{1,0:T(8,128)} %param.30) | copy-start | bytes 13828
  217.9 2.9 %copy-start.6 = (f32[72,128]{1,0:T(8,128)S(1)}, f32[72,128]{1,0:T(8,128)}, u32[]{:S(2)}) copy-start(f32[72,128]{1,0:T(8,128)} %param.20) | copy-start | bytes 110596
  217.9 2.9 %copy-start.8 = (f32[72,128]{1,0:T(8,128)S(1)}, f32[72,128]{1,0:T(8,128)}, u32[]{:S(2)}) copy-start(f32[72,128]{1,0:T(8,128)} %param.23) | copy-start | bytes 110596
  217.9 2.9 %copy-start.12 = (f32[72,128]{1,0:T(8,128)S(1)}, f32[72,128]{1,0:T(8,128)}, u32[]{:S(2)}) copy-start(f32[72,128]{1,0:T(8,128)} %param.25) | copy-start | bytes 110596
  217.9 2.8 %copy-start.13 = (f32[72,128]{1,0:T(8,128)S(1)}, f32[72,128]{1,0:T(8,128)}, u32[]{:S(2)}) copy-start(f32[72,128]{1,0:T(8,128)} %param.24) | copy-start | bytes 110596
  217.9 2.8 %copy-start.14 = (f32[72,128]{1,0:T(8,128)S(1)}, f32[72,128]{1,0:T(8,128)}, u32[]{:S(2)}) copy-start(f32[72,128]{1,0:T(8,128)} %param.22) | copy-start | bytes 110596
  217.9 2.8 %copy-start.15 = (f32[72,128]{1,0:T(8,128)S(1)}, f32[72,128]{1,0:T(8,128)}, u32[]{:S(2)}) copy-start(f32[72,128]{1,0:T(8,128)} %param.21) | copy-start | bytes 110596
  (3 other events, 3.5 us)

commit v3 on v2

--- a/solution.py
+++ b/solution.py
@@ -422,8 +422,20 @@
     extra = item_ref[0, 1:2, :]
     mean, var, mu, rstd = stat(4), stat(5), stat(6), stat(7)
     mean_v = alpha * (mean + vec(3)) + extra
+    products = weight_grad(x2t_ref, 0, pc_ref, acc_ref, 1)
     sb, sx, sg, mean_en, c1, c2, c3, total = norm_back(
-        pc_ref, t2_ref, conv_ref, d_ref, mean, mean_v, mu, rstd, alpha, vec(6), vec(7)
+        pc_ref,
+        t2_ref,
+        conv_ref,
+        d_ref,
+        mean,
+        mean_v,
+        mu,
+        rstd,
+        alpha,
+        vec(6),
+        vec(7),
+        products[:3],
     )
     d_scaling = (
         rstd * (vec(6) * sx - mean_en * (rstd * alpha * PIX) * var) + (mean + vec(3)) * total
@@ -440,7 +452,7 @@
         put_padded(pd_ref, j, d_ref[j, at, :] * c1 + (x * c3 + c2), y0, small)
 
     run(
-        weight_grad(x2t_ref, 0, pc_ref, acc_ref, 1),
+        products[3:],
         [part(spread, *c) for c in chunks(small)],
     )
     wrap_rows(pd_ref)
@@ -457,7 +469,7 @@
             dk_ref[...] += before_ref[...]
 
 
-def norm_back(p_ref, t_ref, src_ref, d_ref, mean, mean_v, mu, rstd, alpha, gain, beta):
+def norm_back(p_ref, t_ref, src_ref, d_ref, mean, mean_v, mu, rstd, alpha, gain, beta, others=()):
     big = 8
     slope = rstd * alpha
     centre = (mean_v - mu) * rstd
@@ -477,7 +489,7 @@
             sums[0] = sums[0] + rows8(d)
             sums[1] = sums[1] + rows8(d * x)
 
-    run([functools.partial(conv, q, y0) for q in range(2) for y0 in range(0, H, big)])
+    run([functools.partial(conv, q, y0) for q in range(2) for y0 in range(0, H, big)], others)
     sb = jnp.sum(sums[0], axis=0, keepdims=True)
     sx = jnp.sum(sums[1], axis=0, keepdims=True) - mean * sb
     sg = slope * sx + centre * sb
@@ -624,10 +636,9 @@
 
     def to_peer(x, hops, start, count, after=None):
         at = lax.rem(me + hops, groups) * items + start
-        part = lax.dynamic_slice_in_dim(x, at, count, 0)
         if after is not None:
-            part, _ = lax.optimization_barrier((part, after))
-        return swap(part, "grp", hops)
+            x, _ = lax.optimization_barrier((x, after))
+        return swap(lax.dynamic_slice_in_dim(x, at, count, 0), "grp", hops)
 
     field_parts = [masked_low] + [to_peer(masked_low, s, 0, items) for s in range(1, groups)]
     share = mid_weight.shape[0]

time: 222 us -> 221 us (level)
    dynamic_slice x2 -> x3, local copies, waits for them, and re-layouts: 4.79 us -> 6.5 us  [to_peer(): return swap(lax.dynamic_slice_in_dim(x, at, count, 0), 'grp', hops)]
  transfers between devices with their start and end apart: 13 -> 13, of which waited for: 6 -> 6; matrix products, arithmetic and copies ran while one was open for 11% -> 12% of each run, Pallas kernels for 69% -> 69%
where the time goes in v3:
time: 221 us
  Pallas kernels  153 us (69%)
  starting transfers between devices  23.3 us (11%)
  other arithmetic  19.5 us (9%)
  waiting for transfers between devices  11.5 us (5%)
  local copies, waits for them, and re-layouts  11.3 us (5%)
    pallas_call x2, Pallas kernels, local(): pl.pallas_call(functools.partial(first_back_kernel, groups, some, chained...  64.2 us
    pallas_call x1, Pallas kernels, local(): pl.pallas_call(functools.partial(forward_kernel, groups, early_steps), gr...  50.1 us
    pallas_call x1, Pallas kernels, local(): pl.pallas_call(functools.partial(second_back_kernel, groups), grid=(items...  38.6 us
    ppermute x6, starting transfers between devices, swap(): return lax.ppermute(x, axis, [(i, (i + hops) % size) for i in range(size)])  8.01 us
    dynamic_update_slice x2, other arithmetic, local(): lax.dynamic_update_slice(block_out, block.astype(f32), (source + start, 0...  6.6 us
    dynamic_slice x3, local copies, waits for them, and re-layouts, to_peer(): return swap(lax.dynamic_slice_in_dim(x, at, count, 0), 'grp', hops)  6.5 us
    ppermute x5, starting transfers between devices, all_sum(): x = x + lax.ppermute(x, axis, [(i, i ^ bit) for i in range(size)])  6.39 us
    ppermute x5, waiting for transfers between devices, all_sum(): x = x + lax.ppermute(x, axis, [(i, i ^ bit) for i in range(size)])  5.16 us
  transfers between devices with their start and end apart: 13, of which 6 were waited for; matrix products, arithmetic and copies ran while one was open for 12% of the time, Pallas kernels for 69%

profile of v3, /device:TPU:0, one launch (start us, length us, event | category | flops | bytes accessed | tf_op | source)
XLA Modules:
  0.0 220.5 jit_solution(16121677481101395104)
XLA Ops:
  1.4 1.3 multiply_convert_fusion.refs_0_
  2.8 3.0 %collective-permute-start = (bf16[8,8,2048]{2,1,0:T(8,128)(2,1)S(1)}, bf16[8,8,2048]{2,1,0:T(8,128)(2,1)S(1)}, u32[]{:S(2)}, u32[]{:S(2)}) collective-permute-start(bf16[8,8,2048]{2,1,0:T(8,128)(2,1)S(1)} %constant_dynamic-slice_fusion.2), channel_id=1, source_target_pairs={{0,1},{1,0},{2,3},{3,2},{4,5},{5,4},{6,7},{7,6},{8,9},{9,8},{10,11... | collective-permute-start | bytes 786440 | tf_op jit(solution)/shard_map/ppermute | solution.py:590
  5.9 0.9 broadcast_in_dim.6
  6.8 4.9 %all-to-all-start = ((bf16[32,72,128]{2,1,0:T(8,128)(2,1)}), bf16[32,72,128]{2,1,0:T(8,128)(2,1)S(1)}, u32[]{:S(2)}, u32[]{:S(2)}) async-start(bf16[32,72,128]{2,1,0:T(8,128)(2,1)} %broadcast_in_dim.6), calls=%async_computation | async-start | bytes 1179648 | tf_op jit(solution)/shard_map/all_to_all | solution.py:646
  11.7 3.2 %constant_dynamic-slice_fusion = bf16[4,64,4096]{2,1,0:T(8,128)(2,1)} fusion(bf16[16,64,4096]{2,1,0:T(8,128)(2,1)} %refs_2_.3, s32[]{:T(128)S(6)} %select_n.70), kind=kLoop, calls=%fused_computation.77 | loop fusion | bytes 4194308 | tf_op jit(solution)/shard_map/dynamic_slice | solution.py:641
  14.9 1.8 collective-permute-start.2
  19.6 0.9 fusion.3.refs_2_.perm_ref
  20.5 3.2 %constant_dynamic-slice_fusion.1 = bf16[4,64,4096]{2,1,0:T(8,128)(2,1)} fusion(bf16[16,64,4096]{2,1,0:T(8,128)(2,1)} %refs_2_.3, s32[]{:T(128)S(6)} %select_n.76), kind=kLoop, calls=%fused_computation.78 | loop fusion | bytes 4194308 | tf_op jit(solution)/shard_map/dynamic_slice | solution.py:641
  24.0 4.0 %all-to-all-done = bf16[32,72,128]{2,1,0:T(8,128)(2,1)S(1)} async-done(((bf16[32,72,128]{2,1,0:T(8,128)(2,1)}), bf16[32,72,128]{2,1,0:T(8,128)(2,1)S(1)}, u32[]{:S(2)}, u32[]{:S(2)}) %all-to-all-start) | async-done | bytes 589856 | tf_op jit(solution)/shard_map/all_to_all | solution.py:646
  28.1 0.8 copy-done.1
  28.9 50.1 %forward_items.1 = (bf16[8,4,1024,128]{3,2,1,0:T(8,128)(2,1)}, bf16[8,4,1024,128]{3,2,1,0:T(8,128)(2,1)}, bf16[8,2,256,1024]{3,2,1,0:T(8,128)(2,1)}, bf16[8,2,25...) custom-call(s32[1]{0:T(128)} %bitcast.me_ref, ...), custom_call_target="tpu_custom_call" | custom-call | flops 40587440128 | bytes 62914560 | tf_op jit(solution)/shard_map/forward_items/pallas_call | solution.py:699
  79.0 1.7 collective-permute-start.3
  80.7 31.8 %first_back_items.2 = (bf16[8,6,66,16,128]{4,3,2,1,0:T(8,128)(2,1)}, bf16[8,6,66,16,128]{4,3,2,1,0:T(8,128)(2,1)}, f32[2,1152,128]{2,1,0:T(8,128)}, f32[8,128]{1,0:T(8,128)}, f32[4,8,128]{2,1,0:T(8,128)}) custom-call(s32[1]{0:T(128)} %bitcast.me_ref, bf16[16,64,4096]{2,1,0:T(8,128)(2,1)} %refs_2_.3, ...), custom_call_target="tpu_custom_call" | custom-call | flops 29957396480 | bytes 30198988 | tf_op jit(solution)/shard_map/first_back_items/pallas_call | solution.py:774
  112.6 0.7 constant_dynamic-update-slice_fusion.1
  113.3 32.4 %first_back_items.3 = (bf16[8,6,66,16,128]{4,3,2,1,0:T(8,128)(2,1)}, bf16[8,6,66,16,128]{4,3,2,1,0:T(8,128)(2,1)}, f32[2,1152,128]{2,1,0:T(8,128)}, f32[8,128]{1,0:T(8,128)}, f32[4,8,128]{2,1,0:T(8,128)}) custom-call(s32[1]{0:T(128)} %bitcast.me_ref, bf16[16,64,4096]{2,1,0:T(8,128)(2,1)} %refs_2_.3, ...), custom_call_target="tpu_custom_call", output_to_operand_aliasing={{0}: (12, {}), {1}: (13, {})} | custom-call | flops 29957396480 | bytes 30198988 | tf_op jit(solution)/shard_map/first_back_items/pallas_call | solution.py:774
  146.4 0.7 constant_dynamic-update-slice_fusion
  147.2 2.5 %pad_maximum_fusion = f32[16,176,128]{2,1,0:T(8,128)} fusion(f32[16,32,128]{2,1,0:T(8,128)S(1)} %broadcast_in_dim.7, f32[16,144,128]{2,1,0:T(8,128)} %bitcast.52), kind=kLoop, calls=%fused_computation.2 | loop fusion | flops 360448 | bytes 2883584 | tf_op jit(solution)/shard_map/concatenate | solution.py:825
  149.7 4.0 %all-to-all-start.1 = ((f32[16,176,128]{2,1,0:T(8,128)}), f32[16,176,128]{2,1,0:T(8,128)S(1)}, u32[]{:S(2)}, u32[]{:S(2)}) async-start(f32[16,176,128]{2,1,0:T(8,128)} %pad_maximum_fusion), calls=%async_computation.1 | async-start | bytes 2883584 | tf_op jit(solution)/shard_map/all_to_all | solution.py:826
  154.2 2.3 %collective-permute-done.3 = bf16[4,64,4096]{2,1,0:T(8,128)(2,1)S(1)} collective-permute-done((bf16[4,64,4096]{2,1,0:T(8,128)(2,1)}, bf16[4,64,4096]{2,1,0:T(8,128)(2,1)S(1)}, u32[]{:S(2)}, u32[]{:S(2)}) %collective-permute-start.3) | collective-permute-done | bytes 2097184 | tf_op jit(solution)/shard_map/ppermute | solution.py:590
  156.5 38.6 %second_back_items.1 = (bf16[2,8,8,2048]{3,2,1,0:T(8,128)(2,1)}, f32[144,512]{1,0:T(8,128)}, f32[8,128]{1,0:T(8,128)}) custom-call(bf16[8,6,66,16,128]{4,3,2,1,0:T(8,128)(2,1)} %get-tuple-element.57.pc_ref, bf16[8,6,66,16,128]{4,3,2,1,0:T(8,128)(2,1)} %get-tuple-element.58.pd_ref, bf16[8,4,1024,128]{3,2,1,0:T(8,128)(2,1)} %get-tuple-element.59.lifted_ref, ...), custom_call_target="tpu_custom_call" | custom-call | flops 23192823808 | bytes 38587596 | tf_op jit(solution)/shard_map/second_back_items/pallas_call | solution.py:829
  195.1 0.8 slice_add_fusion
  197.9 1.2 collective-permute-start.5
  199.1 0.7 collective-permute-start.9
  199.8 2.1 collective-permute-done.5
  201.9 1.7 collective-permute-start.6
  203.7 2.5 %convert_dynamic-update-slice_fusion.1 = f32[16,64,4096]{2,1,0:T(8,128)} fusion(f32[16,64,4096]{2,1,0:T(8,128)} %get-tuple-element.48, s32[]{:T(128)S(6)} %select_n.70, bf16[4,64,4096]{2,1,0:T(8,128)(2,1)S(1)} %collective-permute-done.3), kind=kLoop, calls=%fused_computation.1 | loop fusion | flops 1048576 | bytes 6291460 | tf_op jit(solution)/shard_map/dynamic_update_slice | solution.py:896
  206.2 2.5 %collective-permute-start.7 = (f32[80,128]{1,0:T(8,128)S(1)}, f32[80,128]{1,0:T(8,128)S(1)}, u32[]{:S(2)}, u32[]{:S(2)}) collective-permute-start(f32[80,128]{1,0:T(8,128)S(1)} %add.250), channel_id=1, source_target_pairs={{0,16},{2,18},{4,20},{6,22},{8,24},{10,26},{12,28},{14,30},{16,0},... | collective-permute-start | bytes 122888 | tf_op jit(solution)/shard_map/ppermute | solution.py:597
  208.8 2.3 %collective-permute-done.7 = f32[80,128]{1,0:T(8,128)S(1)} collective-permute-done((f32[80,128]{1,0:T(8,128)S(1)}, f32[80,128]{1,0:T(8,128)S(1)}, u32[]{:S(2)}, u32[]{:S(2)}) %collective-permute-start.7) | collective-permute-done | bytes 40992 | tf_op jit(solution)/shard_map/ppermute | solution.py:597
  211.8 1.0 collective-permute-start.10
  212.8 4.1 %convert_dynamic-update-slice_fusion = f32[16,64,4096]{2,1,0:T(8,128)} fusion(f32[16,64,4096]{2,1,0:T(8,128)} %convert_dynamic-update-slice_fusion.1, s32[]{:T(128)S(6)} %select_n.76, bf16[4,64,4096]{2,1,0:T(8,128)(2,1)} %collective-permute-done.8), kind=kLoop, calls=%fused_computation | loop fusion | flops 1048576 | bytes 6291460 | tf_op jit(solution)/shard_map/dynamic_update_slice | solution.py:896
  217.0 1.1 broadcast_multiply_fusion
  218.3 0.8 multiply_subtract_fusion
  (104 shorter events, 9.5 us)
Async XLA Ops:
  0.6 5.2 %copy-start.7 = (f32[72,128]{1,0:T(8,128)S(1)}, f32[72,128]{1,0:T(8,128)}, u32[]{:S(2)}) copy-start(f32[72,128]{1,0:T(8,128)} %param.23) | copy-start | bytes 110596
  2.8 12.2 %copy-start = (bf16[16,8,2048]{2,1,0:T(8,128)(2,1)}, bf16[16,8,2048]{2,1,0:T(8,128)(2,1)S(1)}, u32[]{:S(2)}) copy-start(bf16[16,8,2048]{2,1,0:T(8,128)(2,1)S(1)} %multiply_convert_fusion.refs_0_) | copy-start | bytes 1572868
  2.8 17.7 %collective-permute-start = (bf16[8,8,2048]{2,1,0:T(8,128)(2,1)S(1)}, bf16[8,8,2048]{2,1,0:T(8,128)(2,1)S(1)}, u32[]{:S(2)}, u32[]{:S(2)}) collective-permute-start(bf16[8,8,2048]{2,1,0:T(8,128)(2,1)S(1)} %constant_dynamic-slice_fusion.2), channel_id=1, source_target_pairs={{0,1},{1,0},{2,3},{3,2},{4,5},{5,4},{6,7},{7,6},{8,9},{9,8},{10,11... | collective-permute-start | bytes 786440 | tf_op jit(solution)/shard_map/ppermute | solution.py:590
  6.8 21.3 %all-to-all-start = ((bf16[32,72,128]{2,1,0:T(8,128)(2,1)}), bf16[32,72,128]{2,1,0:T(8,128)(2,1)S(1)}, u32[]{:S(2)}, u32[]{:S(2)}) async-start(bf16[32,72,128]{2,1,0:T(8,128)(2,1)} %broadcast_in_dim.6), calls=%async_computation | async-start | bytes 1179648 | tf_op jit(solution)/shard_map/all_to_all | solution.py:646
  11.7 5.1 %copy-start.11 = (f32[9,128]{1,0:T(8,128)S(1)}, f32[9,128]{1,0:T(8,128)}, u32[]{:S(2)}) copy-start(f32[9,128]{1,0:T(8,128)} %param.29) | copy-start | bytes 13828
  11.7 5.1 %copy-start.21 = (s32[16]{0:T(128)S(1)}, s32[16]{0:T(128)}, u32[]{:S(2)}) copy-start(s32[16]{0:T(128)} %param.18) | copy-start | bytes 196
  11.7 5.2 %copy-start.2 = (f32[128,256]{1,0:T(8,128)S(1)}, f32[128,256]{1,0:T(8,128)}, u32[]{:S(2)}) copy-start(f32[128,256]{1,0:T(8,128)} %param.26) | copy-start | bytes 393220
  11.7 5.9 %copy-start.5 = (f32[72,128]{1,0:T(8,128)S(1)}, f32[72,128]{1,0:T(8,128)}, u32[]{:S(2)}) copy-start(f32[72,128]{1,0:T(8,128)} %param.20) | copy-start | bytes 110596
  14.9 65.8 %collective-permute-start.2 = (bf16[4,64,4096]{2,1,0:T(8,128)(2,1)}, bf16[4,64,4096]{2,1,0:T(8,128)(2,1)}, u32[]{:S(2)}, u32[]{:S(2)}) collective-permute-start(bf16[4,64,4096]{2,1,0:T(8,128)(2,1)} %constant_dynamic-slice_fusion), channel_id=1, source_target_pairs={{0,1},{1,0},{2,3},{3,2},{4,5},{5,4},{6,7},{7,6},{8,9},{9,8},{10,11... | collective-permute-start | bytes 6291464 | tf_op jit(solution)/shard_map/ppermute | solution.py:590
  20.5 3.3 %copy-start.20 = (bf16[8,8,2048]{2,1,0:T(8,128)(2,1)}, bf16[8,8,2048]{2,1,0:T(8,128)(2,1)S(1)}, u32[]{:S(2)}) copy-start(bf16[8,8,2048]{2,1,0:T(8,128)(2,1)S(1)} %collective-permute-done.refs_1_) | copy-start | bytes 786436
  23.8 89.5 %collective-permute-start.1 = (bf16[4,64,4096]{2,1,0:T(8,128)(2,1)}, bf16[4,64,4096]{2,1,0:T(8,128)(2,1)}, u32[]{:S(2)}, u32[]{:S(2)}) collective-permute-start(bf16[4,64,4096]{2,1,0:T(8,128)(2,1)} %constant_dynamic-slice_fusion.1), channel_id=1, source_target_pairs={{0,1},{1,0},{2,3},{3,2},{4,5},{5,4},{6,7},{7,6},{8,9},{9,8},{10,11... | collective-permute-start | bytes 6291464 | tf_op jit(solution)/shard_map/ppermute | solution.py:590
  79.0 77.5 %collective-permute-start.3 = (bf16[4,64,4096]{2,1,0:T(8,128)(2,1)}, bf16[4,64,4096]{2,1,0:T(8,128)(2,1)S(1)}, u32[]{:S(2)}, u32[]{:S(2)}) collective-permute-start(bf16[4,64,4096]{2,1,0:T(8,128)(2,1)} %get-tuple-element.61), channel_id=1, source_target_pairs={{0,1},{1,0},{2,3},{3,2},{4,5},{5,4},{6,7},{7,6},{8,9},{9,8},{10,11... | collective-permute-start | bytes 6291464 | tf_op jit(solution)/shard_map/ppermute | solution.py:590
  113.3 32.4 %copy-start.19 = (f32[8,128]{1,0:T(8,128)S(1)}, f32[8,128]{1,0:T(8,128)}, u32[]{:S(2)}) copy-start(f32[8,128]{1,0:T(8,128)} %get-tuple-element.67) | copy-start | bytes 12292
  149.7 45.4 %all-to-all-start.1 = ((f32[16,176,128]{2,1,0:T(8,128)}), f32[16,176,128]{2,1,0:T(8,128)S(1)}, u32[]{:S(2)}, u32[]{:S(2)}) async-start(f32[16,176,128]{2,1,0:T(8,128)} %pad_maximum_fusion), calls=%async_computation.1 | async-start | bytes 2883584 | tf_op jit(solution)/shard_map/all_to_all | solution.py:826
  153.7 57.4 %collective-permute-start.8 = (bf16[4,64,4096]{2,1,0:T(8,128)(2,1)}, bf16[4,64,4096]{2,1,0:T(8,128)(2,1)}, u32[]{:S(2)}, u32[]{:S(2)}) collective-permute-start(bf16[4,64,4096]{2,1,0:T(8,128)(2,1)} %get-tuple-element.75), channel_id=1, source_target_pairs={{0,1},{1,0},{2,3},{3,2},{4,5},{5,4},{6,7},{7,6},{8,9},{9,8},{10,11... | collective-permute-start | bytes 6291464 | tf_op jit(solution)/shard_map/ppermute | solution.py:590
  196.6 2.4 %copy-start.4 = (bf16[2,8,8,2048]{3,2,1,0:T(8,128)(2,1)S(1)}, bf16[2,8,8,2048]{3,2,1,0:T(8,128)(2,1)}, u32[]{:S(2)}) copy-start(bf16[2,8,8,2048]{3,2,1,0:T(8,128)(2,1)} %get-tuple-element.77) | copy-start | bytes 1572868
  196.6 1.2 collective-permute-start.4
  197.9 4.1 %collective-permute-start.5 = (f32[80,128]{1,0:T(8,128)S(1)}, f32[80,128]{1,0:T(8,128)S(1)}, u32[]{:S(2)}, u32[]{:S(2)}) collective-permute-start(f32[80,128]{1,0:T(8,128)S(1)} %fusion.32), channel_id=1, source_target_pairs={{0,4},{2,6},{4,0},{6,2},{8,12},{10,14},{12,8},{14,10},{16,20},{18,... | collective-permute-start | bytes 122888 | tf_op jit(solution)/shard_map/ppermute | solution.py:597
  199.1 17.8 %collective-permute-start.9 = (bf16[8,8,2048]{2,1,0:T(8,128)(2,1)S(1)}, bf16[8,8,2048]{2,1,0:T(8,128)(2,1)S(1)}, u32[]{:S(2)}, u32[]{:S(2)}) collective-permute-start(bf16[8,8,2048]{2,1,0:T(8,128)(2,1)S(1)} %dynamic-slice_bitcast_fusion), channel_id=1, source_target_pairs={{0,1},{1,0},{2,3},{3,2},{4,5},{5,4},{6,7},{7,6},{8,9},{9,8},{10,11... | collective-permute-start | bytes 786440 | tf_op jit(solution)/shard_map/ppermute | solution.py:590
  201.9 4.2 %collective-permute-start.6 = (f32[80,128]{1,0:T(8,128)S(1)}, f32[80,128]{1,0:T(8,128)S(1)}, u32[]{:S(2)}, u32[]{:S(2)}) collective-permute-start(f32[80,128]{1,0:T(8,128)S(1)} %add.249), channel_id=1, source_target_pairs={{0,8},{2,10},{4,12},{6,14},{8,0},{10,2},{12,4},{14,6},{16,24},{18,... | collective-permute-start | bytes 122888 | tf_op jit(solution)/shard_map/ppermute | solution.py:597
  206.2 5.0 %collective-permute-start.7 = (f32[80,128]{1,0:T(8,128)S(1)}, f32[80,128]{1,0:T(8,128)S(1)}, u32[]{:S(2)}, u32[]{:S(2)}) collective-permute-start(f32[80,128]{1,0:T(8,128)S(1)} %add.250), channel_id=1, source_target_pairs={{0,16},{2,18},{4,20},{6,22},{8,24},{10,26},{12,28},{14,30},{16,0},... | collective-permute-start | bytes 122888 | tf_op jit(solution)/shard_map/ppermute | solution.py:597
  211.8 6.4 %collective-permute-start.10 = (f32[488,128]{1,0:T(8,128)S(1)}, f32[488,128]{1,0:T(8,128)S(1)}, u32[]{:S(2)}, u32[]{:S(2)}) collective-permute-start(f32[488,128]{1,0:T(8,128)S(1)} %constant_dynamic-update-slice_fusion.2), channel_id=1, source_target_pairs={{0,1},{1,0},{2,3},{3,2},{4,5},{5,4},{6,7},{7,6},{8,9},{9,8},{10,11... | collective-permute-start | bytes 749576 | tf_op jit(solution)/shard_map/ppermute | solution.py:597
  216.9 1.4 copy-start.9
  216.9 1.5 copy-start.10
  216.9 2.2 %copy-start.17 = (f32[9,128]{1,0:T(8,128)S(1)}, f32[9,128]{1,0:T(8,128)}, u32[]{:S(2)}) copy-start(f32[9,128]{1,0:T(8,128)} %param.31) | copy-start | bytes 13828
  216.9 2.2 copy-start.18
  217.0 2.8 %copy-start.6 = (f32[72,128]{1,0:T(8,128)S(1)}, f32[72,128]{1,0:T(8,128)}, u32[]{:S(2)}) copy-start(f32[72,128]{1,0:T(8,128)} %param.20) | copy-start | bytes 110596
  217.0 2.8 %copy-start.8 = (f32[72,128]{1,0:T(8,128)S(1)}, f32[72,128]{1,0:T(8,128)}, u32[]{:S(2)}) copy-start(f32[72,128]{1,0:T(8,128)} %param.23) | copy-start | bytes 110596
  217.0 2.8 %copy-start.12 = (f32[72,128]{1,0:T(8,128)S(1)}, f32[72,128]{1,0:T(8,128)}, u32[]{:S(2)}) copy-start(f32[72,128]{1,0:T(8,128)} %param.25) | copy-start | bytes 110596
  217.0 2.8 %copy-start.13 = (f32[72,128]{1,0:T(8,128)S(1)}, f32[72,128]{1,0:T(8,128)}, u32[]{:S(2)}) copy-start(f32[72,128]{1,0:T(8,128)} %param.24) | copy-start | bytes 110596
  217.0 2.8 %copy-start.14 = (f32[72,128]{1,0:T(8,128)S(1)}, f32[72,128]{1,0:T(8,128)}, u32[]{:S(2)}) copy-start(f32[72,128]{1,0:T(8,128)} %param.22) | copy-start | bytes 110596
  217.0 2.8 %copy-start.15 = (f32[72,128]{1,0:T(8,128)S(1)}, f32[72,128]{1,0:T(8,128)}, u32[]{:S(2)}) copy-start(f32[72,128]{1,0:T(8,128)} %param.21) | copy-start | bytes 110596
  (3 other events, 3.5 us)
